TPU v7x, 32 devices: a whole 2x2x4 slice. The times are simulated.
32 devices in a mesh: group: 2 (over x), date: 16 (over z, y, core).
Axes of the slice: x: 2, y: 2, z: 4, core: 2. Of those that a mesh axis runs over, the one named last changes fastest.
Arguments:
- slc_stack: bfloat16 [16, 2, 32, 16384], P('date', None, 'group'), parts along dimension 2, may hold values from -30 to 30
- band_taps: bfloat16 [2, 2, 32], replicated, may hold values from -1 to 1
- pair_flags: int32 [16, 4], P('date'), may hold values from 0 to 1, as said below
Outputs:
- iono_phase: float32 [16, 8, 1024], P('date', 'group'), parts along dimension 1
- weight_sum: float32 [16, 8, 1024], P('date', 'group'), parts along dimension 1
There are 2 independent parts, one for each index of `group`. A program takes and returns all parts, laid end to end along the dimension named above; an argument that names none is the same for every part. Nothing has to cross between parts.
Inputs may be any that keep to these rules, and one draw needn't show every extreme that they name: pair_flags[d,0] is 1 for every date but the last; pair_flags[d,k] is 0 where d + k + 1 >= 16.
All inputs are finite; a program needn't handle non-finite values.
Results may differ from a plain program's by a relative error of at most 0.002.
Values may be sent and summed in bfloat16 or wider, within the bound.
A program may use at most 128 MiB of HBM per device.

v0:
```python
import jax
import jax.numpy as jnp
from jax import lax
from jax.sharding import PartitionSpec as P

TAPS = 32
ML_AZ = 4
ML_RG = 16
SPAN = 4
RADIUS = 8
ITERS = 4


eps_power = 1e-06
floor_weight = 0.1
ridge_weight = 0.05
split_coef = 2.0


def shifted(value, axis, steps):
    count = lax.axis_size(axis)
    first, last = (max(0, -steps), min(count, count - steps))
    return lax.ppermute(value, axis, [(source, source + steps) for source in range(first, last)])


def prefix(part, axis, combine, identity):
    place = lax.axis_index(axis)
    gathered = lax.all_gather(part, axis)
    state = jnp.zeros_like(part) + jnp.asarray(identity, part.dtype)

    def one(lap, state):
        return combine(state, lax.dynamic_index_in_dim(gathered, lap, 0, False))

    return lax.fori_loop(0, place, one, state)


def tap_matrix(band_taps):
    coeffs = band_taps.astype(jnp.float32)
    column = lax.broadcasted_iota(jnp.int32, (TAPS, 256, 128), 2)
    source = lax.broadcasted_iota(jnp.int32, (TAPS, 256, 128), 1)
    lagged = lax.broadcasted_iota(jnp.int32, (TAPS, 256, 128), 0)
    selector = (source - column == lagged).astype(jnp.float32)
    toeplitz = jnp.einsum("bru,uji->brji", coeffs, selector)
    upper_half = jnp.stack([toeplitz[:, 0], toeplitz[:, 1]], axis=1)
    bottom = jnp.stack([-toeplitz[:, 1], toeplitz[:, 0]], axis=1)
    matrix = jnp.stack([upper_half, bottom], axis=0)
    return matrix.transpose(0, 3, 1, 2, 4).reshape(512, 512).astype(jnp.bfloat16)


def split_bands(one_scene, matrix):
    row_count = one_scene.shape[1]
    blocks = one_scene.shape[2] // 128
    left_pad = TAPS // 2
    padded = jnp.pad(one_scene, ((0, 0), (0, 0), (left_pad, 128 - left_pad)))
    pieces = padded.reshape(2, row_count, blocks + 1, 128)
    windows = jnp.concatenate([pieces[:, :, :-1], pieces[:, :, 1:]], axis=3)
    windows = windows.transpose(1, 2, 0, 3).reshape(row_count, blocks, 512)
    filtered = jnp.dot(windows, matrix, preferred_element_type=jnp.float32)
    return filtered.astype(jnp.bfloat16).reshape(row_count, blocks, 2, 2, 128)


def multilook(values):
    row_count = values.shape[0]
    blocks = values.shape[1]
    groups = 128 // ML_RG
    summed = values.reshape(row_count // ML_AZ, ML_AZ, blocks, 2, groups, ML_RG).sum(axis=(1, 5))
    return summed.transpose(2, 0, 1, 3).reshape(2, row_count // ML_AZ, blocks * groups)


def band_power(bands):
    real_part = bands[:, :, :, 0].astype(jnp.float32)
    imag_part = bands[:, :, :, 1].astype(jnp.float32)
    return multilook(real_part * real_part + imag_part * imag_part)


def local(slc_stack, band_taps, pair_flags):
    own_scene = slc_stack[0]
    matrix = tap_matrix(band_taps)
    own_bands = split_bands(own_scene, matrix)
    own_power = band_power(own_bands)
    flags = pair_flags[0].astype(jnp.float32)
    looks_wide = own_power.shape[2]
    row_ids = lax.broadcasted_iota(jnp.int32, (looks_wide, looks_wide), 0)
    col_ids = lax.broadcasted_iota(jnp.int32, (looks_wide, looks_wide), 1)
    box_matrix = (jnp.abs(row_ids - col_ids) <= RADIUS).astype(jnp.float32)
    own_real = own_bands[:, :, :, 0].astype(jnp.float32)
    own_imag = own_bands[:, :, :, 1].astype(jnp.float32)
    smooth_list = []
    phase_list = []
    for offset in range(1, SPAN + 1):
        far_scene = shifted(own_scene, "date", -offset)
        partner = split_bands(far_scene, matrix)
        partner_real = partner[:, :, :, 0].astype(jnp.float32)
        partner_imag = partner[:, :, :, 1].astype(jnp.float32)
        cross_real = multilook(own_real * partner_real + own_imag * partner_imag)
        cross_imag = multilook(own_imag * partner_real - own_real * partner_imag)
        partner_power = band_power(partner)
        coherence = (cross_real * cross_real + cross_imag * cross_imag) / (
            own_power * partner_power + eps_power
        )
        weight = flags[offset - 1] * 0.5 * (coherence[0] + coherence[1])
        normalizer = jnp.sqrt(
            (own_power[0] * partner_power[0] + eps_power)
            * (own_power[1] * partner_power[1] + eps_power)
        )
        cross_term = cross_imag[0] * cross_real[1] - cross_real[0] * cross_imag[1]
        raw_phase = split_coef * cross_term / normalizer
        stacked = jnp.concatenate([weight * raw_phase, weight], axis=0)
        smoothed = jnp.matmul(stacked, box_matrix, precision=lax.Precision.HIGHEST)
        look_rows = weight.shape[0]
        numerator = smoothed[:look_rows]
        denominator = smoothed[look_rows:]
        phase_list.append(numerator / (denominator + floor_weight))
        smooth_list.append(denominator / (2 * RADIUS + 1))
    chain_start = prefix(
        phase_list[0], "date", lambda former, latter: former + latter, jnp.zeros_like(phase_list[0])
    )
    low_weight = []
    low_phase = []
    for offset in range(1, SPAN + 1):
        packed = jnp.stack([smooth_list[offset - 1], phase_list[offset - 1]], axis=0)
        received = shifted(packed, "date", offset)
        low_weight.append(received[0])
        low_phase.append(received[1])
    weight_sum = jnp.zeros_like(chain_start)
    for offset in range(1, SPAN + 1):
        weight_sum = weight_sum + smooth_list[offset - 1] + low_weight[offset - 1]
    diagonal = weight_sum + ridge_weight
    iono_phase = chain_start
    for sweep_index in range(ITERS):
        accumulated = ridge_weight * chain_start
        for offset in range(1, SPAN + 1):
            later_value = shifted(iono_phase, "date", -offset)
            earlier_value = shifted(iono_phase, "date", offset)
            accumulated = accumulated + smooth_list[offset - 1] * (
                later_value - phase_list[offset - 1]
            )
            accumulated = accumulated + low_weight[offset - 1] * (
                earlier_value + low_phase[offset - 1]
            )
        iono_phase = accumulated / diagonal
    return (iono_phase[None], weight_sum[None])


def solution(mesh):
    in_specs = (P("date", None, "group", None), P(), P("date", None))
    out_specs = (P("date", "group", None), P("date", "group", None))
    return jax.shard_map(local, mesh=mesh, in_specs=in_specs, out_specs=out_specs, check_vma=False)
```

profile of v0, /device:TPU:0, one launch (start us, length us, event | category | flops | bytes accessed | tf_op | source)
XLA Modules:
  0.0 306.0 jit_solution(17553632208209028197)
XLA Ops:
  12.2 2.6 convolution_convert_fusion.4
  14.8 2.5 reshape.355
  17.4 4.2 %fusion.85 = (bf16[16,128,2,1,128]{4,3,2,1,0:T(2,128)(2,1)}, bf16[16,128,2,1,128]{4,3,2,1,0:T(2,128)(2,1)}) fusion(bf16[16,128,2,2,128]{4,3,2,1,0:T(2,128)(2,1)S(1)} %reshape.355), kind=kLoop, calls=%fused_computation.173 | loop fusion | bytes 4194304 | tf_op jit(solution)/shard_map/slice | solution.py:87
  21.6 4.7 %copy.54 = bf16[16,128,2,1,128]{1,4,2,0,3:T(8,128)(2,1)S(1)} copy(bf16[16,128,2,1,128]{4,3,2,1,0:T(2,128)(2,1)} %get-tuple-element.62) | data formatting | bytes 2097152
  26.4 3.4 %copy.56 = bf16[16,128,2,1,128]{1,4,2,0,3:T(8,128)(2,1)} copy(bf16[16,128,2,1,128]{4,3,2,1,0:T(2,128)(2,1)S(1)} %copy-done.4) | data formatting | bytes 2097152
  36.8 2.6 convolution_convert_fusion.3
  39.4 2.5 reshape.358
  42.0 4.2 %fusion.86 = (bf16[16,128,2,1,128]{4,3,2,1,0:T(2,128)(2,1)}, bf16[16,128,2,1,128]{4,3,2,1,0:T(2,128)(2,1)}) fusion(bf16[16,128,2,2,128]{4,3,2,1,0:T(2,128)(2,1)S(1)} %reshape.358), kind=kLoop, calls=%fused_computation.174 | loop fusion | bytes 4194304 | tf_op jit(solution)/shard_map/slice | solution.py:94
  50.3 2.7 convolution_convert_fusion.1
  52.9 2.5 reshape.364
  55.5 4.2 %fusion.83 = (bf16[16,128,2,1,128]{4,3,2,1,0:T(2,128)(2,1)}, bf16[16,128,2,1,128]{4,3,2,1,0:T(2,128)(2,1)}) fusion(bf16[16,128,2,2,128]{4,3,2,1,0:T(2,128)(2,1)S(1)} %reshape.364), kind=kLoop, calls=%fused_computation.171 | loop fusion | bytes 4194304 | tf_op jit(solution)/shard_map/slice | solution.py:94
  59.7 14.1 %collective-permute-done.12 = bf16[2,16,16384]{2,1,0:T(8,128)(2,1)} collective-permute-done((bf16[2,16,16384]{2,1,0:T(8,128)(2,1)}, bf16[2,16,16384]{2,1,0:T(8,128)(2,1)}, u32[]{:S(2)}, u32[]{:S(2)}) %collective-permute-start.12) | collective-permute-done | bytes 1048608 | tf_op jit(solution)/shard_map/ppermute | solution.py:23
  78.0 2.6 convolution_convert_fusion
  80.7 5.9 %copy.55 = bf16[16,128,2,1,128]{1,4,2,0,3:T(8,128)(2,1)} copy(bf16[16,128,2,1,128]{4,3,2,1,0:T(2,128)(2,1)} %get-tuple-element.64) | data formatting | bytes 2097152
  86.6 3.4 %copy.57 = bf16[16,128,2,1,128]{1,4,2,0,3:T(8,128)(2,1)} copy(bf16[16,128,2,1,128]{4,3,2,1,0:T(2,128)(2,1)S(1)} %copy-done.2) | data formatting | bytes 2097152
  90.0 5.9 %copy.60 = bf16[16,128,2,1,128]{1,4,2,0,3:T(8,128)(2,1)} copy(bf16[16,128,2,1,128]{4,3,2,1,0:T(2,128)(2,1)} %get-tuple-element.58) | data formatting | bytes 2097152
  95.9 3.4 %copy.61 = bf16[16,128,2,1,128]{1,4,2,0,3:T(8,128)(2,1)} copy(bf16[16,128,2,1,128]{4,3,2,1,0:T(2,128)(2,1)S(1)} %copy-done.3) | data formatting | bytes 2097152
  99.3 2.5 reshape.367
  101.8 4.2 %fusion.84 = (bf16[16,128,2,1,128]{4,3,2,1,0:T(2,128)(2,1)}, bf16[16,128,2,1,128]{4,3,2,1,0:T(2,128)(2,1)}) fusion(bf16[16,128,2,2,128]{4,3,2,1,0:T(2,128)(2,1)S(1)} %reshape.367), kind=kLoop, calls=%fused_computation.172 | loop fusion | bytes 4194304 | tf_op jit(solution)/shard_map/slice | solution.py:94
  106.1 5.9 %copy.62 = bf16[16,128,2,1,128]{1,4,2,0,3:T(8,128)(2,1)} copy(bf16[16,128,2,1,128]{4,3,2,1,0:T(2,128)(2,1)} %get-tuple-element.60) | data formatting | bytes 2097152
  112.0 3.3 %copy.63 = bf16[16,128,2,1,128]{1,4,2,0,3:T(8,128)(2,1)} copy(bf16[16,128,2,1,128]{4,3,2,1,0:T(2,128)(2,1)S(1)} %copy-done.5) | data formatting | bytes 2097152
  119.4 2.6 convolution_convert_fusion.2
  122.0 2.5 reshape.361
  124.6 4.2 %fusion.82 = (bf16[16,128,2,1,128]{4,3,2,1,0:T(2,128)(2,1)}, bf16[16,128,2,1,128]{4,3,2,1,0:T(2,128)(2,1)}) fusion(bf16[16,128,2,2,128]{4,3,2,1,0:T(2,128)(2,1)S(1)} %reshape.361), kind=kLoop, calls=%fused_computation.170 | loop fusion | bytes 4194304 | tf_op jit(solution)/shard_map/slice | solution.py:94
  128.8 5.9 %copy.58 = bf16[16,128,2,1,128]{1,4,2,0,3:T(8,128)(2,1)} copy(bf16[16,128,2,1,128]{4,3,2,1,0:T(2,128)(2,1)} %get-tuple-element.56) | data formatting | bytes 2097152
  134.7 3.3 %copy.59 = bf16[16,128,2,1,128]{1,4,2,0,3:T(8,128)(2,1)} copy(bf16[16,128,2,1,128]{4,3,2,1,0:T(2,128)(2,1)S(1)} %copy-done.6) | data formatting | bytes 2097152
  138.1 11.7 %fusion.10 = (f32[16,128,2,1,128]{1,4,2,0,3:T(8,128)}, f32[16,128,2,1,128]{1,4,2,0,3:T(8,128)}, f32[16,128,2,1,128]{1,4,2,0,3:T(8,128)}, f32[16,128,2,1,128]{1,4...) fusion(bf16[16,128,2,1,128]{1,4,2,0,3:T(8,128)(2,1)} %copy.58, ...), kind=kLoop, calls=%fused_computation.38 | loop fusion | flops 25690112 | bytes 37748736 | tf_op jit(solution)/shard_map/add | solution.py:95
  173.2 17.8 %all-gather.1 = f32[16,4,1024]{2,1,0:T(4,128)S(1)} all-gather(f32[1,4,1024]{2,1,0:T(4,128)S(1)} %bitcast.251), channel_id=2, replica_groups=mesh['group'=2,'date'=16] {'date'}, dimensions={0}, use_global_device_ids=true | all-gather | bytes 278528 | tf_op jit(solution)/shard_map/all_gather | solution.py:28
  192.4 4.7 %collective-permute-start.11 = (f32[4,1024]{1,0:T(4,128)S(1)}, f32[4,1024]{1,0:T(4,128)S(1)}, u32[]{:S(2)}, u32[]{:S(2)}) collective-permute-start(f32[4,1024]{1,0:T(4,128)S(1)} %get-tuple-element.25), channel_id=1, source_target_pairs={{0,3},{1,4},{2,5},{3,6},{4,7},{5,8},{6,9},{7,10},{8,11},{9,12},{10... | collective-permute-start | bytes 49160 | tf_op jit(solution)/shard_map/ppermute | solution.py:23
  198.4 4.5 %collective-permute-start.15 = (f32[4,1024]{1,0:T(4,128)S(1)}, f32[4,1024]{1,0:T(4,128)S(1)}, u32[]{:S(2)}, u32[]{:S(2)}) collective-permute-start(f32[4,1024]{1,0:T(4,128)S(1)} %get-tuple-element.25), channel_id=1, source_target_pairs={{0,4},{1,5},{2,6},{3,7},{4,8},{5,9},{6,10},{7,11},{8,12},{9,13},{1... | collective-permute-start | bytes 49160 | tf_op jit(solution)/shard_map/ppermute | solution.py:23
  202.9 2.8 collective-permute-start.3
  210.7 4.5 %collective-permute-start.7 = (f32[4,1024]{1,0:T(4,128)S(1)}, f32[4,1024]{1,0:T(4,128)S(1)}, u32[]{:S(2)}, u32[]{:S(2)}) collective-permute-start(f32[4,1024]{1,0:T(4,128)S(1)} %get-tuple-element.25), channel_id=1, source_target_pairs={{0,2},{1,3},{2,4},{3,5},{4,6},{5,7},{6,8},{7,9},{8,10},{9,11},{10,... | collective-permute-start | bytes 49160 | tf_op jit(solution)/shard_map/ppermute | solution.py:23
  215.3 2.4 collective-permute-start.14
  217.7 3.1 %collective-permute-start.10 = (f32[2,4,1024]{2,1,0:T(4,128)S(1)}, f32[2,4,1024]{2,1,0:T(4,128)S(1)}, u32[]{:S(2)}, u32[]{:S(2)}) collective-permute-start(f32[2,4,1024]{2,1,0:T(4,128)S(1)} %pad_maximum_fusion.2), channel_id=1, source_target_pairs={{0,3},{1,4},{2,5},{3,6},{4,7},{5,8},{6,9},{7,10},{8,11},{9,12},{10... | collective-permute-start | bytes 98312 | tf_op jit(solution)/shard_map/ppermute | solution.py:23
  220.9 2.5 collective-permute-start.6
  226.2 3.8 %collective-permute-done.9 = f32[4,1024]{1,0:T(4,128)S(1)} collective-permute-done((f32[4,1024]{1,0:T(4,128)S(1)}, f32[4,1024]{1,0:T(4,128)S(1)}, u32[]{:S(2)}, u32[]{:S(2)}) %collective-permute-start.9) | collective-permute-done | bytes 16416 | tf_op jit(solution)/shard_map/ppermute | solution.py:23
  231.3 4.3 %collective-permute-start.17 = (f32[4,1024]{1,0:T(4,128)S(1)}, f32[4,1024]{1,0:T(4,128)S(1)}, u32[]{:S(2)}, u32[]{:S(2)}) collective-permute-start(f32[4,1024]{1,0:T(4,128)S(1)} %get-tuple-element.34), channel_id=1, source_target_pairs={{0,1},{1,2},{2,3},{3,4},{4,5},{5,6},{6,7},{7,8},{8,9},{9,10},{10,1... | collective-permute-start | bytes 49160 | tf_op jit(solution)/shard_map/ppermute | solution.py:23
  236.9 4.5 %collective-permute-start.19 = (f32[4,1024]{1,0:T(4,128)S(1)}, f32[4,1024]{1,0:T(4,128)S(1)}, u32[]{:S(2)}, u32[]{:S(2)}) collective-permute-start(f32[4,1024]{1,0:T(4,128)S(1)} %get-tuple-element.34), channel_id=1, source_target_pairs={{0,2},{1,3},{2,4},{3,5},{4,6},{5,7},{6,8},{7,9},{8,10},{9,11},{10,... | collective-permute-start | bytes 49160 | tf_op jit(solution)/shard_map/ppermute | solution.py:23
  242.8 5.7 %collective-permute-start.21 = (f32[4,1024]{1,0:T(4,128)S(1)}, f32[4,1024]{1,0:T(4,128)S(1)}, u32[]{:S(2)}, u32[]{:S(2)}) collective-permute-start(f32[4,1024]{1,0:T(4,128)S(1)} %get-tuple-element.34), channel_id=1, source_target_pairs={{0,3},{1,4},{2,5},{3,6},{4,7},{5,8},{6,9},{7,10},{8,11},{9,12},{10... | collective-permute-start | bytes 49160 | tf_op jit(solution)/shard_map/ppermute | solution.py:23
  249.8 4.5 %collective-permute-start.23 = (f32[4,1024]{1,0:T(4,128)S(1)}, f32[4,1024]{1,0:T(4,128)S(1)}, u32[]{:S(2)}, u32[]{:S(2)}) collective-permute-start(f32[4,1024]{1,0:T(4,128)S(1)} %get-tuple-element.34), channel_id=1, source_target_pairs={{0,4},{1,5},{2,6},{3,7},{4,8},{5,9},{6,10},{7,11},{8,12},{9,13},{1... | collective-permute-start | bytes 49160 | tf_op jit(solution)/shard_map/ppermute | solution.py:23
  257.2 3.0 collective-permute-start.25
  261.5 4.5 %collective-permute-start.27 = (f32[4,1024]{1,0:T(4,128)S(1)}, f32[4,1024]{1,0:T(4,128)S(1)}, u32[]{:S(2)}, u32[]{:S(2)}) collective-permute-start(f32[4,1024]{1,0:T(4,128)S(1)} %add_divide_fusion.6), channel_id=1, source_target_pairs={{0,2},{1,3},{2,4},{3,5},{4,6},{5,7},{6,8},{7,9},{8,10},{9,11},{10,... | collective-permute-start | bytes 49160 | tf_op jit(solution)/shard_map/ppermute | solution.py:23
  267.4 5.9 %collective-permute-start.29 = (f32[4,1024]{1,0:T(4,128)S(1)}, f32[4,1024]{1,0:T(4,128)S(1)}, u32[]{:S(2)}, u32[]{:S(2)}) collective-permute-start(f32[4,1024]{1,0:T(4,128)S(1)} %add_divide_fusion.6), channel_id=1, source_target_pairs={{0,3},{1,4},{2,5},{3,6},{4,7},{5,8},{6,9},{7,10},{8,11},{9,12},{10... | collective-permute-start | bytes 49160 | tf_op jit(solution)/shard_map/ppermute | solution.py:23
  274.6 4.5 %collective-permute-start.31 = (f32[4,1024]{1,0:T(4,128)S(1)}, f32[4,1024]{1,0:T(4,128)S(1)}, u32[]{:S(2)}, u32[]{:S(2)}) collective-permute-start(f32[4,1024]{1,0:T(4,128)S(1)} %add_divide_fusion.6), channel_id=1, source_target_pairs={{0,4},{1,5},{2,6},{3,7},{4,8},{5,9},{6,10},{7,11},{8,12},{9,13},{1... | collective-permute-start | bytes 49160 | tf_op jit(solution)/shard_map/ppermute | solution.py:23
  281.9 3.0 collective-permute-start.33
  286.3 5.0 %collective-permute-start.35 = (f32[4,1024]{1,0:T(4,128)S(1)}, f32[4,1024]{1,0:T(4,128)S(1)}, u32[]{:S(2)}, u32[]{:S(2)}) collective-permute-start(f32[4,1024]{1,0:T(4,128)S(1)} %add_divide_fusion.5), channel_id=1, source_target_pairs={{0,2},{1,3},{2,4},{3,5},{4,6},{5,7},{6,8},{7,9},{8,10},{9,11},{10,... | collective-permute-start | bytes 49160 | tf_op jit(solution)/shard_map/ppermute | solution.py:23
  292.6 5.4 %collective-permute-start.37 = (f32[4,1024]{1,0:T(4,128)S(1)}, f32[4,1024]{1,0:T(4,128)S(1)}, u32[]{:S(2)}, u32[]{:S(2)}) collective-permute-start(f32[4,1024]{1,0:T(4,128)S(1)} %add_divide_fusion.5), channel_id=1, source_target_pairs={{0,3},{1,4},{2,5},{3,6},{4,7},{5,8},{6,9},{7,10},{8,11},{9,12},{10... | collective-permute-start | bytes 49160 | tf_op jit(solution)/shard_map/ppermute | solution.py:23
  299.3 4.5 %collective-permute-start.39 = (f32[4,1024]{1,0:T(4,128)S(1)}, f32[4,1024]{1,0:T(4,128)S(1)}, u32[]{:S(2)}, u32[]{:S(2)}) collective-permute-start(f32[4,1024]{1,0:T(4,128)S(1)} %add_divide_fusion.5), channel_id=1, source_target_pairs={{0,4},{1,5},{2,6},{3,7},{4,8},{5,9},{6,10},{7,11},{8,12},{9,13},{1... | collective-permute-start | bytes 49160 | tf_op jit(solution)/shard_map/ppermute | solution.py:23
  (177 shorter events, 82.3 us)
Async XLA Ops:
  0.6 5.2 %copy-start = (bf16[2,2,32]{2,1,0:T(2,128)(2,1)S(1)}, bf16[2,2,32]{2,1,0:T(2,128)(2,1)}, u32[]{:S(2)}) copy-start(bf16[2,2,32]{2,1,0:T(2,128)(2,1)} %param.6) | copy-start | bytes 772
  0.6 32.1 %collective-permute-start = (bf16[2,16,16384]{2,1,0:T(8,128)(2,1)}, bf16[2,16,16384]{2,1,0:T(8,128)(2,1)}, u32[]{:S(2)}, u32[]{:S(2)}) collective-permute-start(bf16[2,16,16384]{2,1,0:T(8,128)(2,1)} %bitcast.244), channel_id=1, source_target_pairs={{1,0},{2,1},{3,2},{4,3},{5,4},{6,5},{7,6},{8,7},{9,8},{10,9},{11,1... | collective-permute-start | bytes 3145736 | tf_op jit(solution)/shard_map/ppermute | solution.py:23
  1.9 44.3 %collective-permute-start.8 = (bf16[2,16,16384]{2,1,0:T(8,128)(2,1)}, bf16[2,16,16384]{2,1,0:T(8,128)(2,1)}, u32[]{:S(2)}, u32[]{:S(2)}) collective-permute-start(bf16[2,16,16384]{2,1,0:T(8,128)(2,1)} %bitcast.245), channel_id=1, source_target_pairs={{3,0},{4,1},{5,2},{6,3},{7,4},{8,5},{9,6},{10,7},{11,8},{12,9},{13... | collective-permute-start | bytes 3145736 | tf_op jit(solution)/shard_map/ppermute | solution.py:23
  3.2 70.5 %collective-permute-start.12 = (bf16[2,16,16384]{2,1,0:T(8,128)(2,1)}, bf16[2,16,16384]{2,1,0:T(8,128)(2,1)}, u32[]{:S(2)}, u32[]{:S(2)}) collective-permute-start(bf16[2,16,16384]{2,1,0:T(8,128)(2,1)} %bitcast.246), channel_id=1, source_target_pairs={{4,0},{5,1},{6,2},{7,3},{8,4},{9,5},{10,6},{11,7},{12,8},{13,9},{1... | collective-permute-start | bytes 3145736 | tf_op jit(solution)/shard_map/ppermute | solution.py:23
  4.5 110.8 %collective-permute-start.4 = (bf16[2,16,16384]{2,1,0:T(8,128)(2,1)}, bf16[2,16,16384]{2,1,0:T(8,128)(2,1)}, u32[]{:S(2)}, u32[]{:S(2)}) collective-permute-start(bf16[2,16,16384]{2,1,0:T(8,128)(2,1)} %bitcast.247), channel_id=1, source_target_pairs={{2,0},{3,1},{4,2},{5,3},{6,4},{7,5},{8,6},{9,7},{10,8},{11,9},{12,... | collective-permute-start | bytes 3145736 | tf_op jit(solution)/shard_map/ppermute | solution.py:23
  21.6 4.8 %copy-start.4 = (bf16[16,128,2,1,128]{4,3,2,1,0:T(2,128)(2,1)S(1)}, bf16[16,128,2,1,128]{4,3,2,1,0:T(2,128)(2,1)}, u32[]{:S(2)}) copy-start(bf16[16,128,2,1,128]{4,3,2,1,0:T(2,128)(2,1)} %get-tuple-element.61) | copy-start | bytes 3145732
  80.7 5.9 %copy-start.2 = (bf16[16,128,2,1,128]{4,3,2,1,0:T(2,128)(2,1)S(1)}, bf16[16,128,2,1,128]{4,3,2,1,0:T(2,128)(2,1)}, u32[]{:S(2)}) copy-start(bf16[16,128,2,1,128]{4,3,2,1,0:T(2,128)(2,1)} %get-tuple-element.63) | copy-start | bytes 3145732
  90.0 5.9 %copy-start.3 = (bf16[16,128,2,1,128]{4,3,2,1,0:T(2,128)(2,1)S(1)}, bf16[16,128,2,1,128]{4,3,2,1,0:T(2,128)(2,1)}, u32[]{:S(2)}) copy-start(bf16[16,128,2,1,128]{4,3,2,1,0:T(2,128)(2,1)} %get-tuple-element.57) | copy-start | bytes 3145732
  106.1 5.9 %copy-start.5 = (bf16[16,128,2,1,128]{4,3,2,1,0:T(2,128)(2,1)S(1)}, bf16[16,128,2,1,128]{4,3,2,1,0:T(2,128)(2,1)}, u32[]{:S(2)}) copy-start(bf16[16,128,2,1,128]{4,3,2,1,0:T(2,128)(2,1)} %get-tuple-element.59) | copy-start | bytes 3145732
  128.8 5.9 %copy-start.6 = (bf16[16,128,2,1,128]{4,3,2,1,0:T(2,128)(2,1)S(1)}, bf16[16,128,2,1,128]{4,3,2,1,0:T(2,128)(2,1)}, u32[]{:S(2)}) copy-start(bf16[16,128,2,1,128]{4,3,2,1,0:T(2,128)(2,1)} %get-tuple-element.55) | copy-start | bytes 3145732
  191.1 18.3 %collective-permute-start.1 = (f32[4,1024]{1,0:T(4,128)S(1)}, f32[4,1024]{1,0:T(4,128)S(1)}, u32[]{:S(2)}, u32[]{:S(2)}) collective-permute-start(f32[4,1024]{1,0:T(4,128)S(1)} %get-tuple-element.25), channel_id=1, source_target_pairs={{1,0},{2,1},{3,2},{4,3},{5,4},{6,5},{7,6},{8,7},{9,8},{10,9},{11,1... | collective-permute-start | bytes 49160 | tf_op jit(solution)/shard_map/ppermute | solution.py:23
  192.4 18.4 %collective-permute-start.11 = (f32[4,1024]{1,0:T(4,128)S(1)}, f32[4,1024]{1,0:T(4,128)S(1)}, u32[]{:S(2)}, u32[]{:S(2)}) collective-permute-start(f32[4,1024]{1,0:T(4,128)S(1)} %get-tuple-element.25), channel_id=1, source_target_pairs={{0,3},{1,4},{2,5},{3,6},{4,7},{5,8},{6,9},{7,10},{8,11},{9,12},{10... | collective-permute-start | bytes 49160 | tf_op jit(solution)/shard_map/ppermute | solution.py:23
  197.1 18.2 %collective-permute-start.13 = (f32[4,1024]{1,0:T(4,128)S(1)}, f32[4,1024]{1,0:T(4,128)S(1)}, u32[]{:S(2)}, u32[]{:S(2)}) collective-permute-start(f32[4,1024]{1,0:T(4,128)S(1)} %get-tuple-element.25), channel_id=1, source_target_pairs={{4,0},{5,1},{6,2},{7,3},{8,4},{9,5},{10,6},{11,7},{12,8},{13,9},{1... | collective-permute-start | bytes 49160 | tf_op jit(solution)/shard_map/ppermute | solution.py:23
  198.4 19.3 %collective-permute-start.15 = (f32[4,1024]{1,0:T(4,128)S(1)}, f32[4,1024]{1,0:T(4,128)S(1)}, u32[]{:S(2)}, u32[]{:S(2)}) collective-permute-start(f32[4,1024]{1,0:T(4,128)S(1)} %get-tuple-element.25), channel_id=1, source_target_pairs={{0,4},{1,5},{2,6},{3,7},{4,8},{5,9},{6,10},{7,11},{8,12},{9,13},{1... | collective-permute-start | bytes 49160 | tf_op jit(solution)/shard_map/ppermute | solution.py:23
  202.9 17.9 %collective-permute-start.3 = (f32[4,1024]{1,0:T(4,128)S(1)}, f32[4,1024]{1,0:T(4,128)S(1)}, u32[]{:S(2)}, u32[]{:S(2)}) collective-permute-start(f32[4,1024]{1,0:T(4,128)S(1)} %get-tuple-element.25), channel_id=1, source_target_pairs={{0,1},{1,2},{2,3},{3,4},{4,5},{5,6},{6,7},{7,8},{8,9},{9,10},{10,1... | collective-permute-start | bytes 49160 | tf_op jit(solution)/shard_map/ppermute | solution.py:23
  208.8 97.2 %copy-start.1 = (bf16[2,2,32]{2,1,0:T(2,128)(2,1)S(1)}, bf16[2,2,32]{2,1,0:T(2,128)(2,1)}, u32[]{:S(2)}) copy-start(bf16[2,2,32]{2,1,0:T(2,128)(2,1)} %param.6) | copy-start | bytes 772
  209.4 14.0 %collective-permute-start.5 = (f32[4,1024]{1,0:T(4,128)S(1)}, f32[4,1024]{1,0:T(4,128)S(1)}, u32[]{:S(2)}, u32[]{:S(2)}) collective-permute-start(f32[4,1024]{1,0:T(4,128)S(1)} %get-tuple-element.25), channel_id=1, source_target_pairs={{2,0},{3,1},{4,2},{5,3},{6,4},{7,5},{8,6},{9,7},{10,8},{11,9},{12,... | collective-permute-start | bytes 49160 | tf_op jit(solution)/shard_map/ppermute | solution.py:23
  210.7 14.1 %collective-permute-start.7 = (f32[4,1024]{1,0:T(4,128)S(1)}, f32[4,1024]{1,0:T(4,128)S(1)}, u32[]{:S(2)}, u32[]{:S(2)}) collective-permute-start(f32[4,1024]{1,0:T(4,128)S(1)} %get-tuple-element.25), channel_id=1, source_target_pairs={{0,2},{1,3},{2,4},{3,5},{4,6},{5,7},{6,8},{7,9},{8,10},{9,11},{10,... | collective-permute-start | bytes 49160 | tf_op jit(solution)/shard_map/ppermute | solution.py:23
  215.3 14.6 %collective-permute-start.14 = (f32[2,4,1024]{2,1,0:T(4,128)S(1)}, f32[2,4,1024]{2,1,0:T(4,128)S(1)}, u32[]{:S(2)}, u32[]{:S(2)}) collective-permute-start(f32[2,4,1024]{2,1,0:T(4,128)S(1)} %pad_maximum_fusion.3), channel_id=1, source_target_pairs={{0,4},{1,5},{2,6},{3,7},{4,8},{5,9},{6,10},{7,11},{8,12},{9,13},{1... | collective-permute-start | bytes 98312 | tf_op jit(solution)/shard_map/ppermute | solution.py:23
  217.7 12.2 %collective-permute-start.10 = (f32[2,4,1024]{2,1,0:T(4,128)S(1)}, f32[2,4,1024]{2,1,0:T(4,128)S(1)}, u32[]{:S(2)}, u32[]{:S(2)}) collective-permute-start(f32[2,4,1024]{2,1,0:T(4,128)S(1)} %pad_maximum_fusion.2), channel_id=1, source_target_pairs={{0,3},{1,4},{2,5},{3,6},{4,7},{5,8},{6,9},{7,10},{8,11},{9,12},{10... | collective-permute-start | bytes 98312 | tf_op jit(solution)/shard_map/ppermute | solution.py:23
  220.9 9.0 %collective-permute-start.6 = (f32[2,4,1024]{2,1,0:T(4,128)S(1)}, f32[2,4,1024]{2,1,0:T(4,128)S(1)}, u32[]{:S(2)}, u32[]{:S(2)}) collective-permute-start(f32[2,4,1024]{2,1,0:T(4,128)S(1)} %pad_maximum_fusion.1), channel_id=1, source_target_pairs={{0,2},{1,3},{2,4},{3,5},{4,6},{5,7},{6,8},{7,9},{8,10},{9,11},{10,... | collective-permute-start | bytes 98312 | tf_op jit(solution)/shard_map/ppermute | solution.py:23
  223.4 6.6 %collective-permute-start.2 = (f32[2,4,1024]{2,1,0:T(4,128)S(1)}, f32[2,4,1024]{2,1,0:T(4,128)S(1)}, u32[]{:S(2)}, u32[]{:S(2)}) collective-permute-start(f32[2,4,1024]{2,1,0:T(4,128)S(1)} %pad_maximum_fusion), channel_id=1, source_target_pairs={{0,1},{1,2},{2,3},{3,4},{4,5},{5,6},{6,7},{7,8},{8,9},{9,10},{10,1... | collective-permute-start | bytes 98312 | tf_op jit(solution)/shard_map/ppermute | solution.py:23
  224.9 5.1 %collective-permute-start.9 = (f32[4,1024]{1,0:T(4,128)S(1)}, f32[4,1024]{1,0:T(4,128)S(1)}, u32[]{:S(2)}, u32[]{:S(2)}) collective-permute-start(f32[4,1024]{1,0:T(4,128)S(1)} %get-tuple-element.25), channel_id=1, source_target_pairs={{3,0},{4,1},{5,2},{6,3},{7,4},{8,5},{9,6},{10,7},{11,8},{12,9},{13... | collective-permute-start | bytes 49160 | tf_op jit(solution)/shard_map/ppermute | solution.py:23
  230.0 75.9 %copy-start.13 = (f32[4,1024]{1,0:T(4,128)}, f32[4,1024]{1,0:T(4,128)S(1)}, u32[]{:S(2)}) copy-start(f32[4,1024]{1,0:T(4,128)S(1)} %get-tuple-element.35) | copy-start | bytes 49156
  230.0 12.7 %collective-permute-start.16 = (f32[4,1024]{1,0:T(4,128)S(1)}, f32[4,1024]{1,0:T(4,128)S(1)}, u32[]{:S(2)}, u32[]{:S(2)}) collective-permute-start(f32[4,1024]{1,0:T(4,128)S(1)} %get-tuple-element.34), channel_id=1, source_target_pairs={{1,0},{2,1},{3,2},{4,3},{5,4},{6,5},{7,6},{8,7},{9,8},{10,9},{11,1... | collective-permute-start | bytes 49160 | tf_op jit(solution)/shard_map/ppermute | solution.py:23
  231.3 17.2 %collective-permute-start.17 = (f32[4,1024]{1,0:T(4,128)S(1)}, f32[4,1024]{1,0:T(4,128)S(1)}, u32[]{:S(2)}, u32[]{:S(2)}) collective-permute-start(f32[4,1024]{1,0:T(4,128)S(1)} %get-tuple-element.34), channel_id=1, source_target_pairs={{0,1},{1,2},{2,3},{3,4},{4,5},{5,6},{6,7},{7,8},{8,9},{9,10},{10,1... | collective-permute-start | bytes 49160 | tf_op jit(solution)/shard_map/ppermute | solution.py:23
  235.6 14.2 %collective-permute-start.18 = (f32[4,1024]{1,0:T(4,128)S(1)}, f32[4,1024]{1,0:T(4,128)S(1)}, u32[]{:S(2)}, u32[]{:S(2)}) collective-permute-start(f32[4,1024]{1,0:T(4,128)S(1)} %get-tuple-element.34), channel_id=1, source_target_pairs={{2,0},{3,1},{4,2},{5,3},{6,4},{7,5},{8,6},{9,7},{10,8},{11,9},{12,... | collective-permute-start | bytes 49160 | tf_op jit(solution)/shard_map/ppermute | solution.py:23
  236.9 17.5 %collective-permute-start.19 = (f32[4,1024]{1,0:T(4,128)S(1)}, f32[4,1024]{1,0:T(4,128)S(1)}, u32[]{:S(2)}, u32[]{:S(2)}) collective-permute-start(f32[4,1024]{1,0:T(4,128)S(1)} %get-tuple-element.34), channel_id=1, source_target_pairs={{0,2},{1,3},{2,4},{3,5},{4,6},{5,7},{6,8},{7,9},{8,10},{9,11},{10,... | collective-permute-start | bytes 49160 | tf_op jit(solution)/shard_map/ppermute | solution.py:23
  241.5 12.9 %collective-permute-start.20 = (f32[4,1024]{1,0:T(4,128)S(1)}, f32[4,1024]{1,0:T(4,128)S(1)}, u32[]{:S(2)}, u32[]{:S(2)}) collective-permute-start(f32[4,1024]{1,0:T(4,128)S(1)} %get-tuple-element.34), channel_id=1, source_target_pairs={{3,0},{4,1},{5,2},{6,3},{7,4},{8,5},{9,6},{10,7},{11,8},{12,9},{13... | collective-permute-start | bytes 49160 | tf_op jit(solution)/shard_map/ppermute | solution.py:23
  242.8 11.6 %collective-permute-start.21 = (f32[4,1024]{1,0:T(4,128)S(1)}, f32[4,1024]{1,0:T(4,128)S(1)}, u32[]{:S(2)}, u32[]{:S(2)}) collective-permute-start(f32[4,1024]{1,0:T(4,128)S(1)} %get-tuple-element.34), channel_id=1, source_target_pairs={{0,3},{1,4},{2,5},{3,6},{4,7},{5,8},{6,9},{7,10},{8,11},{9,12},{10... | collective-permute-start | bytes 49160 | tf_op jit(solution)/shard_map/ppermute | solution.py:23
  248.5 5.9 %collective-permute-start.22 = (f32[4,1024]{1,0:T(4,128)S(1)}, f32[4,1024]{1,0:T(4,128)S(1)}, u32[]{:S(2)}, u32[]{:S(2)}) collective-permute-start(f32[4,1024]{1,0:T(4,128)S(1)} %get-tuple-element.34), channel_id=1, source_target_pairs={{4,0},{5,1},{6,2},{7,3},{8,4},{9,5},{10,6},{11,7},{12,8},{13,9},{1... | collective-permute-start | bytes 49160 | tf_op jit(solution)/shard_map/ppermute | solution.py:23
  249.8 6.0 %collective-permute-start.23 = (f32[4,1024]{1,0:T(4,128)S(1)}, f32[4,1024]{1,0:T(4,128)S(1)}, u32[]{:S(2)}, u32[]{:S(2)}) collective-permute-start(f32[4,1024]{1,0:T(4,128)S(1)} %get-tuple-element.34), channel_id=1, source_target_pairs={{0,4},{1,5},{2,6},{3,7},{4,8},{5,9},{6,10},{7,11},{8,12},{9,13},{1... | collective-permute-start | bytes 49160 | tf_op jit(solution)/shard_map/ppermute | solution.py:23
  255.9 11.5 %collective-permute-start.24 = (f32[4,1024]{1,0:T(4,128)S(1)}, f32[4,1024]{1,0:T(4,128)S(1)}, u32[]{:S(2)}, u32[]{:S(2)}) collective-permute-start(f32[4,1024]{1,0:T(4,128)S(1)} %add_divide_fusion.6), channel_id=1, source_target_pairs={{1,0},{2,1},{3,2},{4,3},{5,4},{6,5},{7,6},{8,7},{9,8},{10,9},{11,1... | collective-permute-start | bytes 49160 | tf_op jit(solution)/shard_map/ppermute | solution.py:23
  257.2 16.1 %collective-permute-start.25 = (f32[4,1024]{1,0:T(4,128)S(1)}, f32[4,1024]{1,0:T(4,128)S(1)}, u32[]{:S(2)}, u32[]{:S(2)}) collective-permute-start(f32[4,1024]{1,0:T(4,128)S(1)} %add_divide_fusion.6), channel_id=1, source_target_pairs={{0,1},{1,2},{2,3},{3,4},{4,5},{5,6},{6,7},{7,8},{8,9},{9,10},{10,1... | collective-permute-start | bytes 49160 | tf_op jit(solution)/shard_map/ppermute | solution.py:23
  260.2 14.3 %collective-permute-start.26 = (f32[4,1024]{1,0:T(4,128)S(1)}, f32[4,1024]{1,0:T(4,128)S(1)}, u32[]{:S(2)}, u32[]{:S(2)}) collective-permute-start(f32[4,1024]{1,0:T(4,128)S(1)} %add_divide_fusion.6), channel_id=1, source_target_pairs={{2,0},{3,1},{4,2},{5,3},{6,4},{7,5},{8,6},{9,7},{10,8},{11,9},{12,... | collective-permute-start | bytes 49160 | tf_op jit(solution)/shard_map/ppermute | solution.py:23
  261.5 17.6 %collective-permute-start.27 = (f32[4,1024]{1,0:T(4,128)S(1)}, f32[4,1024]{1,0:T(4,128)S(1)}, u32[]{:S(2)}, u32[]{:S(2)}) collective-permute-start(f32[4,1024]{1,0:T(4,128)S(1)} %add_divide_fusion.6), channel_id=1, source_target_pairs={{0,2},{1,3},{2,4},{3,5},{4,6},{5,7},{6,8},{7,9},{8,10},{9,11},{10,... | collective-permute-start | bytes 49160 | tf_op jit(solution)/shard_map/ppermute | solution.py:23
  266.1 13.1 %collective-permute-start.28 = (f32[4,1024]{1,0:T(4,128)S(1)}, f32[4,1024]{1,0:T(4,128)S(1)}, u32[]{:S(2)}, u32[]{:S(2)}) collective-permute-start(f32[4,1024]{1,0:T(4,128)S(1)} %add_divide_fusion.6), channel_id=1, source_target_pairs={{3,0},{4,1},{5,2},{6,3},{7,4},{8,5},{9,6},{10,7},{11,8},{12,9},{13... | collective-permute-start | bytes 49160 | tf_op jit(solution)/shard_map/ppermute | solution.py:23
  267.4 11.8 %collective-permute-start.29 = (f32[4,1024]{1,0:T(4,128)S(1)}, f32[4,1024]{1,0:T(4,128)S(1)}, u32[]{:S(2)}, u32[]{:S(2)}) collective-permute-start(f32[4,1024]{1,0:T(4,128)S(1)} %add_divide_fusion.6), channel_id=1, source_target_pairs={{0,3},{1,4},{2,5},{3,6},{4,7},{5,8},{6,9},{7,10},{8,11},{9,12},{10... | collective-permute-start | bytes 49160 | tf_op jit(solution)/shard_map/ppermute | solution.py:23
  273.3 5.9 %collective-permute-start.30 = (f32[4,1024]{1,0:T(4,128)S(1)}, f32[4,1024]{1,0:T(4,128)S(1)}, u32[]{:S(2)}, u32[]{:S(2)}) collective-permute-start(f32[4,1024]{1,0:T(4,128)S(1)} %add_divide_fusion.6), channel_id=1, source_target_pairs={{4,0},{5,1},{6,2},{7,3},{8,4},{9,5},{10,6},{11,7},{12,8},{13,9},{1... | collective-permute-start | bytes 49160 | tf_op jit(solution)/shard_map/ppermute | solution.py:23
  274.6 6.0 %collective-permute-start.31 = (f32[4,1024]{1,0:T(4,128)S(1)}, f32[4,1024]{1,0:T(4,128)S(1)}, u32[]{:S(2)}, u32[]{:S(2)}) collective-permute-start(f32[4,1024]{1,0:T(4,128)S(1)} %add_divide_fusion.6), channel_id=1, source_target_pairs={{0,4},{1,5},{2,6},{3,7},{4,8},{5,9},{6,10},{7,11},{8,12},{9,13},{1... | collective-permute-start | bytes 49160 | tf_op jit(solution)/shard_map/ppermute | solution.py:23
  280.6 12.0 %collective-permute-start.32 = (f32[4,1024]{1,0:T(4,128)S(1)}, f32[4,1024]{1,0:T(4,128)S(1)}, u32[]{:S(2)}, u32[]{:S(2)}) collective-permute-start(f32[4,1024]{1,0:T(4,128)S(1)} %add_divide_fusion.5), channel_id=1, source_target_pairs={{1,0},{2,1},{3,2},{4,3},{5,4},{6,5},{7,6},{8,7},{9,8},{10,9},{11,1... | collective-permute-start | bytes 49160 | tf_op jit(solution)/shard_map/ppermute | solution.py:23
  281.9 16.1 %collective-permute-start.33 = (f32[4,1024]{1,0:T(4,128)S(1)}, f32[4,1024]{1,0:T(4,128)S(1)}, u32[]{:S(2)}, u32[]{:S(2)}) collective-permute-start(f32[4,1024]{1,0:T(4,128)S(1)} %add_divide_fusion.5), channel_id=1, source_target_pairs={{0,1},{1,2},{2,3},{3,4},{4,5},{5,6},{6,7},{7,8},{8,9},{9,10},{10,1... | collective-permute-start | bytes 49160 | tf_op jit(solution)/shard_map/ppermute | solution.py:23
  285.0 14.3 %collective-permute-start.34 = (f32[4,1024]{1,0:T(4,128)S(1)}, f32[4,1024]{1,0:T(4,128)S(1)}, u32[]{:S(2)}, u32[]{:S(2)}) collective-permute-start(f32[4,1024]{1,0:T(4,128)S(1)} %add_divide_fusion.5), channel_id=1, source_target_pairs={{2,0},{3,1},{4,2},{5,3},{6,4},{7,5},{8,6},{9,7},{10,8},{11,9},{12,... | collective-permute-start | bytes 49160 | tf_op jit(solution)/shard_map/ppermute | solution.py:23
  286.3 17.6 %collective-permute-start.35 = (f32[4,1024]{1,0:T(4,128)S(1)}, f32[4,1024]{1,0:T(4,128)S(1)}, u32[]{:S(2)}, u32[]{:S(2)}) collective-permute-start(f32[4,1024]{1,0:T(4,128)S(1)} %add_divide_fusion.5), channel_id=1, source_target_pairs={{0,2},{1,3},{2,4},{3,5},{4,6},{5,7},{6,8},{7,9},{8,10},{9,11},{10,... | collective-permute-start | bytes 49160 | tf_op jit(solution)/shard_map/ppermute | solution.py:23
  291.3 12.6 %collective-permute-start.36 = (f32[4,1024]{1,0:T(4,128)S(1)}, f32[4,1024]{1,0:T(4,128)S(1)}, u32[]{:S(2)}, u32[]{:S(2)}) collective-permute-start(f32[4,1024]{1,0:T(4,128)S(1)} %add_divide_fusion.5), channel_id=1, source_target_pairs={{3,0},{4,1},{5,2},{6,3},{7,4},{8,5},{9,6},{10,7},{11,8},{12,9},{13... | collective-permute-start | bytes 49160 | tf_op jit(solution)/shard_map/ppermute | solution.py:23
  292.6 11.3 %collective-permute-start.37 = (f32[4,1024]{1,0:T(4,128)S(1)}, f32[4,1024]{1,0:T(4,128)S(1)}, u32[]{:S(2)}, u32[]{:S(2)}) collective-permute-start(f32[4,1024]{1,0:T(4,128)S(1)} %add_divide_fusion.5), channel_id=1, source_target_pairs={{0,3},{1,4},{2,5},{3,6},{4,7},{5,8},{6,9},{7,10},{8,11},{9,12},{10... | collective-permute-start | bytes 49160 | tf_op jit(solution)/shard_map/ppermute | solution.py:23
  298.0 5.9 %collective-permute-start.38 = (f32[4,1024]{1,0:T(4,128)S(1)}, f32[4,1024]{1,0:T(4,128)S(1)}, u32[]{:S(2)}, u32[]{:S(2)}) collective-permute-start(f32[4,1024]{1,0:T(4,128)S(1)} %add_divide_fusion.5), channel_id=1, source_target_pairs={{4,0},{5,1},{6,2},{7,3},{8,4},{9,5},{10,6},{11,7},{12,8},{13,9},{1... | collective-permute-start | bytes 49160 | tf_op jit(solution)/shard_map/ppermute | solution.py:23
  299.3 6.0 %collective-permute-start.39 = (f32[4,1024]{1,0:T(4,128)S(1)}, f32[4,1024]{1,0:T(4,128)S(1)}, u32[]{:S(2)}, u32[]{:S(2)}) collective-permute-start(f32[4,1024]{1,0:T(4,128)S(1)} %add_divide_fusion.5), channel_id=1, source_target_pairs={{0,4},{1,5},{2,6},{3,7},{4,8},{5,9},{6,10},{7,11},{8,12},{9,13},{1... | collective-permute-start | bytes 49160 | tf_op jit(solution)/shard_map/ppermute | solution.py:23
  (7 other events, 11.3 us)
where the time goes:
time: 310 us; the launch traced here: 306 us
  starting transfers between devices  107 us (35%)
  local copies, waits for them, and re-layouts  101 us (33%)
  other arithmetic  38 us (12%)
  waiting for transfers between devices  22.1 us (7%)
  blocking collectives  17.8 us (6%)
  matrix products  16 us (5%)
  between operations  4.27 us (1%)
    ppermute x40, starting transfers between devices, shifted(): lax.ppermute(value, axis, [(source, source + steps) for source in range(f...  107 us
    unnamed x40, local copies, waits for them, and re-layouts  49.5 us
    reduce_sum x13, other arithmetic, multilook(): values.reshape(row_count // ML_AZ, ML_AZ, blocks, 2, groups, ML_RG)  22.1 us
    ppermute x40, waiting for transfers between devices, shifted(): lax.ppermute(value, axis, [(source, source + steps) for source in range(f...  22.1 us
    all_gather x1, blocking collectives, prefix(): gathered = lax.all_gather(part, axis)  17.8 us
    slice x4, local copies, waits for them, and re-layouts, local(): partner_imag = partner[:, :, :, 1].astype(jnp.float32)  16.8 us
    dot_general x5, matrix products, split_bands(): filtered = jnp.dot(windows, matrix, preferred_element_type=jnp.float32)  13.2 us
    reshape x5, local copies, waits for them, and re-layouts, split_bands(): return filtered.astype(jnp.bfloat16).reshape(row_count, blocks, 2, 2, 128)  12.7 us
  transfers between devices with their start and end apart: 40, of which 5 were waited for; matrix products, arithmetic and copies ran while one was open for 30% of the time, Pallas kernels for 0%

commit v1 on v0

v1 whole, which is shorter than its diff:
```python
import functools

import jax
import jax.numpy as jnp
from jax import lax
from jax.experimental import pallas as pl
from jax.experimental.pallas import tpu as pltpu
from jax.sharding import PartitionSpec as P

TAPS = 32
ML_AZ = 4
ML_RG = 16
SPAN = 4
RADIUS = 8
ITERS = 4

LANES = 128
CELLS = LANES // ML_RG

eps_power = 1e-06
floor_weight = 0.1
ridge_weight = 0.05
split_coef = 2.0

F32 = jnp.float32
BF16 = jnp.bfloat16


def kernel(
    n, n_rg, pieces,
    data_ref, flags_ref, taps_ref, out_ref,
    recv, flags, mat, filt, bands, power, raw_w, raw_n, wgt, phs, phi_a, phi_b,
    rhs, inv, wsum, pack, back,
    send_sem, recv_sem, fsend_sem, frecv_sem, osend_sem, orecv_sem,
):
    me = lax.axis_index("date")
    blocks = pieces - 1
    own_blocks = pieces - 4
    rows_pad = bands.shape[2]
    my_q = lax.rem(me, n_rg)

    barrier = pltpu.get_barrier_semaphore()

    def greet(i, carry):
        other = lax.rem(me + i, n)
        pl.semaphore_signal(
            barrier, inc=1, device_id={"date": other}, device_id_type=pl.DeviceIdType.MESH
        )
        return carry

    lax.fori_loop(1, n, greet, 0)

    own_copy = pltpu.make_async_copy(data_ref.at[me], recv.at[me], recv_sem.at[me])
    own_copy.start()
    own_flags = pltpu.make_async_copy(flags_ref, flags.at[me + SPAN], frecv_sem.at[me])
    own_flags.start()

    pl.semaphore_wait(barrier, n - 1)

    def data_copy(target, slot):
        return pltpu.make_async_remote_copy(
            src_ref=data_ref.at[target], dst_ref=recv.at[me],
            send_sem=send_sem.at[target], recv_sem=recv_sem.at[me],
            device_id={"date": target}, device_id_type=pl.DeviceIdType.MESH,
        )

    def flag_copy(target):
        return pltpu.make_async_remote_copy(
            src_ref=flags_ref, dst_ref=flags.at[me + SPAN],
            send_sem=fsend_sem.at[target], recv_sem=frecv_sem.at[me],
            device_id={"date": target}, device_id_type=pl.DeviceIdType.MESH,
        )

    def send(i, carry):
        target = lax.rem(me + i, n)
        flag_copy(target).start()
        data_copy(target, 0).start()
        return carry

    lax.fori_loop(1, n, send, 0)

    k_id = lax.broadcasted_iota(jnp.int32, (LANES, LANES), 0)
    j_id = lax.broadcasted_iota(jnp.int32, (LANES, LANES), 1)
    circ = []
    for m in range(4):
        base = jnp.broadcast_to(taps_ref[m:m + 1, :], (LANES, LANES))
        circ.append(pltpu.roll(base, 0, 1, stride=1, stride_axis=0))
    for half in range(2):
        keep = (j_id <= k_id) if half == 0 else (j_id > k_id)
        for band in range(2):
            re_part = jnp.where(keep, circ[2 * band], 0.0).astype(BF16)
            im_value = jnp.where(keep, circ[2 * band + 1], 0.0)
            im_part = im_value.astype(BF16)
            im_minus = (-im_value).astype(BF16)
            col = half * 512 + band * 256
            mat[0:128, col:col + 128] = re_part
            mat[0:128, col + 128:col + 256] = im_part
            mat[128:256, col:col + 128] = im_minus
            mat[128:256, col + 128:col + 256] = re_part

    for ref in (bands, power, raw_w, raw_n, wgt, phs, phi_a, phi_b):
        ref[...] = jnp.zeros_like(ref)
    flags[0:SPAN] = jnp.zeros((SPAN,) + flags.shape[1:], F32)

    cell_row = lax.broadcasted_iota(jnp.int32, (CELLS, 4 * LANES), 0)
    lane = lax.broadcasted_iota(jnp.int32, (CELLS, 4 * LANES), 1)
    pick = lax.rem(lane, LANES) // ML_RG == cell_row
    sum_re = jnp.where(pick, 1.0, 0.0).astype(BF16)
    sum_im = jnp.where(pick, jnp.where(lax.rem(lane, 2 * LANES) < LANES, -1.0, 1.0), 0.0).astype(BF16)
    contract = (((1,), (1,)), ((), ()))

    def looks(value, selector):
        high = value.astype(BF16)
        low = (value - high.astype(F32)).astype(BF16)
        both = jnp.concatenate([high, low], axis=1)
        return lax.dot_general(selector, both, contract, preferred_element_type=F32)

    ring = bands.shape[0]

    def one_date(d, carry):
        pltpu.make_async_copy(recv.at[d], recv.at[d], recv_sem.at[d]).wait()
        pltpu.make_async_copy(
            flags.at[d + SPAN], flags.at[d + SPAN], frecv_sem.at[d]
        ).wait()
        filt[...] = jnp.dot(recv[d], mat[...], preferred_element_type=F32)
        slot = lax.rem(d, ring)
        for r in range(ML_AZ):
            first = r * pieces
            value = filt[first:first + blocks, 0:512] + filt[first + 1:first + 1 + blocks, 512:1024]
            bands[slot, r, 0:blocks, :] = value.astype(BF16).astype(F32)
        new_power = []
        for band in range(2):
            total = None
            for r in range(ML_AZ):
                value = bands[slot, r, :, band * 256:band * 256 + 256]
                total = value * value if total is None else total + value * value
            new_power.append(looks(total, sum_re))
            power[slot, band, :, 0:rows_pad] = new_power[band]
        for k in range(1, SPAN + 1):
            early = lax.rem(d + ring - k, ring)
            cross = []
            for band in range(2):
                total_re = None
                total_im = None
                for r in range(ML_AZ):
                    a = bands[early, r, :, band * 256:band * 256 + 256]
                    b = bands[slot, r, :, band * 256:band * 256 + 256]
                    b_swap = jnp.concatenate([b[:, 128:], b[:, :128]], axis=1)
                    total_re = a * b if total_re is None else total_re + a * b
                    total_im = a * b_swap if total_im is None else total_im + a * b_swap
                cross.append((looks(total_re, sum_re), looks(total_im, sum_im)))
            (cr0, ci0), (cr1, ci1) = cross
            ab0 = power[early, 0, :, 0:rows_pad] * new_power[0] + eps_power
            ab1 = power[early, 1, :, 0:rows_pad] * new_power[1] + eps_power
            flag = flags[d - k + SPAN, k - 1:k, 0:rows_pad]
            weight = flag * 0.5 * ((cr0 * cr0 + ci0 * ci0) / ab0 + (cr1 * cr1 + ci1 * ci1) / ab1)
            phase = split_coef * (ci0 * cr1 - cr0 * ci1) / jnp.sqrt(ab0 * ab1)
            raw_w[k - 1, d - k + SPAN, :, 0:rows_pad] = weight
            raw_n[k - 1, d - k + SPAN, :, 0:rows_pad] = weight * phase
        return carry

    lax.fori_loop(0, n, one_date, 0)

    step = min(8, n)
    shape = (step, CELLS, LANES)
    c_id = lax.broadcasted_iota(jnp.int32, shape, 1)
    b_id = lax.broadcasted_iota(jnp.int32, shape, 2)
    cell = CELLS * (own_blocks * my_q - 2 + b_id) + 1 + c_id
    valid = (b_id < blocks) & (cell >= 0) & (cell < n_rg * own_blocks * CELLS)

    def box(value):
        value = jnp.where(valid, value, 0.0)
        prefix = value
        for hop in (1, 2, 4):
            prefix = prefix + jnp.where(c_id >= hop, pltpu.roll(prefix, hop, 1), 0.0)
        whole = jnp.sum(value, axis=1, keepdims=True)
        suffix = whole - prefix + value
        return pltpu.roll(suffix, 1, 2) + whole + pltpu.roll(prefix, LANES - 1, 2)

    def smooth(i, carry):
        at = i * step + SPAN
        for k in range(SPAN):
            den = box(raw_w[k, pl.ds(at, step)])
            num = box(raw_n[k, pl.ds(at, step)])
            phs[k, pl.ds(at, step)] = num / (den + floor_weight)
            wgt[k, pl.ds(at, step)] = den / (2 * RADIUS + 1)
        return carry

    lax.fori_loop(0, n // step, smooth, 0)

    def chain(d, state):
        phi_a[d + SPAN] = state
        return state + phs[0, d + SPAN]

    lax.fori_loop(0, n, chain, jnp.zeros((CELLS, LANES), F32))

    def constants(i, carry):
        at = i * step + SPAN
        total = jnp.zeros(shape, F32)
        acc = ridge_weight * phi_a[pl.ds(at, step)]
        for k in range(1, SPAN + 1):
            w = wgt[k - 1, pl.ds(at, step)]
            low = wgt[k - 1, pl.ds(at - k, step)]
            total = total + w + low
            acc = acc - w * phs[k - 1, pl.ds(at, step)] + low * phs[k - 1, pl.ds(at - k, step)]
        wsum[pl.ds(i * step, step)] = total
        rhs[pl.ds(i * step, step)] = acc
        inv[pl.ds(i * step, step)] = 1.0 / (total + ridge_weight)
        return carry

    lax.fori_loop(0, n // step, constants, 0)

    for sweep in range(ITERS):
        old, new = (phi_a, phi_b) if sweep % 2 == 0 else (phi_b, phi_a)

        def relax(i, carry):
            at = i * step + SPAN
            acc = rhs[pl.ds(i * step, step)]
            for k in range(1, SPAN + 1):
                acc = acc + wgt[k - 1, pl.ds(at, step)] * old[pl.ds(at + k, step)]
                acc = acc + wgt[k - 1, pl.ds(at - k, step)] * old[pl.ds(at - k, step)]
            new[pl.ds(at, step)] = acc * inv[pl.ds(i * step, step)]
            return carry

        lax.fori_loop(0, n // step, relax, 0)
    last = phi_a if ITERS % 2 == 0 else phi_b

    def align(value):
        down = pltpu.roll(value, 1, 1)
        return jnp.where(c_id == 0, pltpu.roll(down, LANES - 1, 2), pltpu.roll(down, LANES - 2, 2))

    def finish(i, carry):
        phase = align(last[pl.ds(i * step + SPAN, step)])
        total = align(wsum[pl.ds(i * step, step)])
        pack[pl.ds(i * step, step)] = jnp.where(b_id < 64, phase, pltpu.roll(total, 64, 2))
        return carry

    lax.fori_loop(0, n // step, finish, 0)

    def out_copy(target):
        return pltpu.make_async_remote_copy(
            src_ref=pack.at[target], dst_ref=back.at[me],
            send_sem=osend_sem.at[target], recv_sem=orecv_sem.at[me],
            device_id={"date": target}, device_id_type=pl.DeviceIdType.MESH,
        )

    own_back = pltpu.make_async_copy(pack.at[me], back.at[me], orecv_sem.at[me])
    own_back.start()

    def send_back(i, carry):
        out_copy(lax.rem(me + i, n)).start()
        return carry

    lax.fori_loop(1, n, send_back, 0)

    def drain(i, carry):
        target = lax.rem(me + i, n)
        data_copy(target, 0).wait_send()
        flag_copy(target).wait_send()
        out_copy(target).wait_send()
        return carry

    lax.fori_loop(1, n, drain, 0)

    def arrive(s, carry):
        pltpu.make_async_copy(back.at[s], back.at[s], orecv_sem.at[s]).wait()
        out_ref[s] = back[s]
        return carry

    lax.fori_loop(0, n, arrive, 0)


def local(slc_stack, band_taps, pair_flags):
    n = lax.axis_size("date")
    rows, span = slc_stack.shape[2:]
    n_az = rows // ML_AZ
    n_rg = n // n_az
    own_blocks = span // LANES // n_rg
    pieces = own_blocks + 4
    rows_pad = -(-(pieces - 1) // 8) * 8
    chunk_rows = ML_AZ * pieces

    x = slc_stack[0].reshape(2, n_az, ML_AZ, span // LANES, LANES).transpose(1, 2, 3, 0, 4)
    x = jnp.pad(x, ((0, 0), (0, 0), (2, 2), (0, 0), (0, 0)))
    chunks = [x[:, :, q * own_blocks:q * own_blocks + pieces] for q in range(n_rg)]
    data = jnp.stack(chunks, axis=1).reshape(n, chunk_rows, 2 * LANES)

    flags = jnp.broadcast_to(
        jnp.pad(pair_flags[0].astype(F32), (0, 8 - SPAN))[:, None], (8, LANES)
    )
    h = band_taps.astype(F32).reshape(4, TAPS)
    taps = jnp.concatenate(
        [h[:, :1], jnp.zeros((4, LANES - TAPS), F32), jnp.flip(h[:, 1:], axis=1)], axis=1
    )
    taps = jnp.pad(taps, ((0, 4), (0, 0)))

    vmem = pl.BlockSpec(memory_space=pltpu.VMEM)
    small = lambda *lead: pltpu.VMEM((*lead, CELLS, LANES), F32)
    ring = SPAN + 1
    sem = pltpu.SemaphoreType.DMA((n,))
    back = pl.pallas_call(
        functools.partial(kernel, n, n_rg, pieces),
        out_shape=jax.ShapeDtypeStruct((n, CELLS, LANES), F32),
        in_specs=[vmem] * 3,
        out_specs=vmem,
        scratch_shapes=[
            pltpu.VMEM((n, chunk_rows, 2 * LANES), BF16),
            small(n + SPAN),
            pltpu.VMEM((256, 1024), BF16),
            pltpu.VMEM((chunk_rows, 1024), F32),
            pltpu.VMEM((ring, ML_AZ, rows_pad, 512), F32),
            small(ring, 2),
            small(SPAN, n + 2 * SPAN),
            small(SPAN, n + 2 * SPAN),
            small(SPAN, n + 2 * SPAN),
            small(SPAN, n + 2 * SPAN),
            small(n + 2 * SPAN),
            small(n + 2 * SPAN),
            small(n),
            small(n),
            small(n),
            small(n),
            small(n),
            sem, sem, sem, sem, sem, sem,
        ],
        compiler_params=pltpu.CompilerParams(
            collective_id=0, has_side_effects=True, vmem_limit_bytes=48 * 1024 * 1024
        ),
    )(data, flags, taps)
    outs = back.reshape(n_az, n_rg, CELLS, 2, LANES // 2)[..., :own_blocks]
    outs = outs.transpose(3, 0, 1, 4, 2).reshape(2, 1, n_az, span // ML_RG)
    return outs[0], outs[1]


def solution(mesh):
    in_specs = (P("date", None, "group", None), P(), P("date", None))
    out_specs = (P("date", "group", None), P("date", "group", None))
    return jax.shard_map(local, mesh=mesh, in_specs=in_specs, out_specs=out_specs, check_vma=False)
```

time: 310 us -> 59 us (0.19); the launches traced: 306 us -> 58.8 us
  starting transfers between devices: 107 us -> 0 us
  local copies, waits for them, and re-layouts: 101 us -> 6.67 us
  Pallas kernels: 0 us -> 49.2 us
  other arithmetic: 38 us -> 2.24 us
  waiting for transfers between devices: 22.1 us -> 0 us
  blocking collectives: 17.8 us -> 0 us
  matrix products: 16 us -> 0 us
  between operations: 4.27 us -> 0.73 us
    ppermute x40 -> x0, starting transfers between devices: 107 us -> none  [shifted(): lax.ppermute(value, axis, [(source, source + steps) for source in range(f...]
    pallas_call x0 -> x1, Pallas kernels: none -> 49.2 us  [local(): pl.pallas_call(functools.partial(kernel, n, n_rg, pieces), out_shape=jax....]
    unnamed x40 -> x6, local copies, waits for them, and re-layouts: 49.5 us -> 1.7 us
    slice x11 -> x3, local copies, waits for them, and re-layouts: 24.7 us -> 0.11 us  [the longest x1 0.07 us: local(): h[:, 1:]]
    reduce_sum x13 -> x0, other arithmetic: 22.1 us -> none  [multilook(): values.reshape(row_count // ML_AZ, ML_AZ, blocks, 2, groups, ML_RG)]
    ppermute x40 -> x0, waiting for transfers between devices: 22.1 us -> none  [shifted(): lax.ppermute(value, axis, [(source, source + steps) for source in range(f...]
    all_gather x1 -> x0, blocking collectives: 17.8 us -> none  [prefix(): gathered = lax.all_gather(part, axis)]
    dot_general x10 -> x0, matrix products: 16 us -> none  [the longest x5 13.2 us: split_bands(): filtered = jnp.dot(windows, matrix, preferred_element_type=jnp.float32)]
  transfers between devices with their start and end apart: 40 -> 0, of which waited for: 5 -> 0; matrix products, arithmetic and copies ran while one was open for 30% -> 0% of each run, Pallas kernels for 0% -> 0%
where the time goes in v1:
time: 59 us; the launch traced here: 58.8 us
  Pallas kernels  49.2 us (83%)
  local copies, waits for them, and re-layouts  6.67 us (11%)
  other arithmetic  2.24 us (4%)
  between operations  0.73 us (1%)
    pallas_call x1, Pallas kernels, local(): pl.pallas_call(functools.partial(kernel, n, n_rg, pieces), out_shape=jax....  49.2 us
    another operation x1, other arithmetic, local(): data = jnp.stack(chunks, axis=1).reshape(n, chunk_rows, 2 * LANES)  2.16 us
    unnamed x6, local copies, waits for them, and re-layouts  1.7 us
    squeeze x2, local copies, waits for them, and re-layouts, local(): return (outs[0], outs[1])  1.53 us

profile of v1, /device:TPU:0, one launch (start us, length us, event | category | flops | bytes accessed | tf_op | source)
XLA Modules:
  0.0 58.8 jit_solution(15768558707561572838)
XLA Ops:
  0.6 1.5 %copy.17 = bf16[4,8,128,128]{3,2,1,0:T(8,128)(2,1)S(1)} copy(bf16[4,8,128,128]{3,1,2,0:T(8,128)(2,1)} %bitcast.35) | data formatting | bytes 2097152
  2.1 1.1 %copy.19 = bf16[2,4,4,128,128]{4,0,3,2,1:T(2,128)(2,1)S(1)} copy(bf16[2,4,4,128,128]{4,3,2,1,0:T(8,128)(2,1)S(1)} %bitcast.33) | data formatting | bytes 2097152 | tf_op jit(solution)/shard_map/reshape;squeeze | solution.py:283
  3.2 1.1 %fusion = (bf16[4,1,4,36,2,128]{5,4,3,2,1,0:T(2,128)(2,1)S(1)}, bf16[4,1,4,36,2,128]{5,4,3,2,1,0:T(2,128)(2,1)S(1)}, bf16[4,1,4,36,2,128]{5,4,3,2,1,0:T(2,128)(2,1)S(1)}, bf16[4,1,4,36,2,128]{5,4,3,2,1,0:T(2,128)(2,1)S(1)}) fusion(bf16[4,4,128,2,128]{4,3,2,1,0:T(2,128)(2,1)S(1)} %bitcast.32), kind=kLoop, calls=%fused_computation.4 | loop fusion | bytes 2818048 | tf_op jit(solution)/shard_map/stack | solution.py:286
  4.3 2.2 %pad_maximum_fusion = bf16[4,4,4,36,2,128]{5,4,3,2,1,0:T(2,128)(2,1)S(1)} fusion(bf16[4,1,4,36,2,128]{5,4,3,2,1,0:T(2,128)(2,1)S(1)} %get-tuple-element.3, bf16[4,1,4,36,2,128]{5,4,3,2,1,0:T(2,128)(2,1)S(1)} %get-tuple-element.4, bf16[4,1,4,36,2,128]{5,4,3,2,1,0:T(2,128)(2,1)S(1)} %get-tuple-element.5, bf16[4,1,4,36,2,128]{5,4,3,2,1,0:T(2,128)(2,1)S(1)} %get-tuple-element.2), kind=kLoop, calls=%fused_computation | loop fusion | flops 1769472 | bytes 2359296 | tf_op jit(solution)/shard_map/stack | solution.py:286
  6.4 0.0 copy-start
  6.4 0.0 copy-start.1
  6.4 0.8 %reshape.23.data_ref = bf16[16,144,256]{2,1,0:T(8,128)(2,1)S(1)} reshape(bf16[4,4,4,36,2,128]{5,4,3,2,1,0:T(2,128)(2,1)S(1)} %pad_maximum_fusion) | data formatting | bytes 2359296 | tf_op jit(solution)/shard_map/reshape | solution.py:286
  7.2 0.0 copy-done
  7.3 0.1 slice.36
  7.3 0.1 rev.4
  7.4 0.1 pad.16.clone
  7.5 0.1 pad_maximum_fusion.1
  7.6 0.0 copy-done.1
  7.6 0.1 broadcast_in_dim.4.flags_ref
  7.7 49.2 %shard_map.50 = f32[16,8,128]{2,1,0:T(8,128)S(1)} custom-call(bf16[16,144,256]{2,1,0:T(8,128)(2,1)S(1)} %reshape.23.data_ref, f32[8,128]{1,0:T(8,128)S(1)} %broadcast_in_dim.4.flags_ref, f32[8,128]{1,0:T(8,128)S(1)} %pad.14.taps_ref), custom_call_target="tpu_custom_call" | custom-call | tf_op jit(solution)/shard_map/pallas_call | solution.py:301
  56.9 0.1 reshape.26
  57.0 0.2 copy.16
  57.3 0.8 %squeeze.7 = f32[1,4,1024]{2,1,0:T(4,128)} reshape(f32[1,4,4,32,8]{4,3,2,1,0:T(8,128)S(1)} %get-tuple-element.7) | data formatting | bytes 32768 | tf_op jit(solution)/shard_map/squeeze | solution.py:332
  58.1 0.8 %squeeze.8 = f32[1,4,1024]{2,1,0:T(4,128)} reshape(f32[1,4,4,32,8]{4,3,2,1,0:T(8,128)S(1)} %get-tuple-element.6) | data formatting | bytes 32768 | tf_op jit(solution)/shard_map/squeeze | solution.py:332
  (6 shorter events, 0.1 us)
Async XLA Ops:
  6.4 0.8 %copy-start = (bf16[2,2,32]{2,1,0:T(2,128)(2,1)S(1)}, bf16[2,2,32]{2,1,0:T(2,128)(2,1)}, u32[]{:S(2)}) copy-start(bf16[2,2,32]{2,1,0:T(2,128)(2,1)} %param.4) | copy-start | bytes 772
  6.4 1.2 %copy-start.1 = (s32[1,4]{1,0:T(1,128)S(1)}, s32[1,4]{1,0:T(1,128)}, u32[]{:S(2)}) copy-start(s32[1,4]{1,0:T(1,128)} %param.5) | copy-start | bytes 52

commit v2 on v1

--- a/solution.py
+++ b/solution.py
@@ -27,11 +27,11 @@
 
 
 def kernel(
-    n, n_rg, pieces,
-    data_ref, flags_ref, taps_ref, out_ref,
-    recv, flags, mat, filt, bands, power, raw_w, raw_n, wgt, phs, phi_a, phi_b,
+    n, n_rg, pieces, cuts,
+    slc_ref, flags_in, taps_ref, out_ref,
+    slc, data, own_flags, recv, flags, mat, filt, bands, power, raw_w, raw_n, wgt, phs, phi_a, phi_b,
     rhs, inv, wsum, pack, back,
-    send_sem, recv_sem, fsend_sem, frecv_sem, osend_sem, orecv_sem,
+    in_sem, send_sem, recv_sem, fsend_sem, frecv_sem, osend_sem, orecv_sem,
 ):
     me = lax.axis_index("date")
     blocks = pieces - 1
@@ -50,41 +50,102 @@
 
     lax.fori_loop(1, n, greet, 0)
 
-    own_copy = pltpu.make_async_copy(data_ref.at[me], recv.at[me], recv_sem.at[me])
-    own_copy.start()
-    own_flags = pltpu.make_async_copy(flags_ref, flags.at[me + SPAN], frecv_sem.at[me])
-    own_flags.start()
-
-    pl.semaphore_wait(barrier, n - 1)
-
-    def data_copy(target, slot):
+    load = pltpu.make_async_copy(slc_ref.at[0], slc, in_sem)
+    load.start()
+
+    row_8 = lax.broadcasted_iota(jnp.int32, (8, 4), 0)
+    col_8 = lax.broadcasted_iota(jnp.int32, (8, 4), 1)
+    picked = jnp.where(row_8 == col_8, flags_in[...].astype(F32), 0.0)
+    own_flags[...] = jnp.broadcast_to(jnp.sum(picked, axis=1, keepdims=True), (8, LANES))
+    load.wait()
+
+    n_az = n // n_rg
+    n_tiles = data.shape[1] // 16
+    n_blocks = slc.shape[2] // LANES
+    upper = lax.broadcasted_iota(jnp.int32, (8, LANES), 0) < ML_AZ
+
+    def regroup(tile, lo, hi):
+        for part in range(2):
+            for half in range(n_az // 2):
+                made = ([], [])
+                for pair in range(2):
+                    two = []
+                    for m in (2 * pair, 2 * pair + 1):
+                        if lo <= m < hi:
+                            at = pl.multiple_of((4 * tile - 2 + m) * LANES, LANES)
+                            value = slc[part, :, pl.ds(at, LANES)].astype(F32)
+                            two.append(value[8 * half:8 * half + 8])
+                        else:
+                            two.append(jnp.zeros((8, LANES), F32))
+                    made[0].append(jnp.where(upper, two[0], pltpu.roll(two[1], ML_AZ, 0)))
+                    made[1].append(jnp.where(upper, pltpu.roll(two[0], ML_AZ, 0), two[1]))
+                for odd in range(2):
+                    value = jnp.concatenate(made[odd], axis=0).astype(BF16)
+                    to = pl.multiple_of(tile * 16, 16)
+                    data[2 * half + odd, pl.ds(to, 16), part * LANES:part * LANES + LANES] = value
+
+    def inner_tile(tile, carry):
+        regroup(tile, 0, 4)
+        return carry
+
+    lax.fori_loop(1, n_tiles - 1, inner_tile, 0, unroll=False)
+    regroup(0, 2, 4)
+    regroup(n_tiles - 1, 0, 2)
+
+    chunk_rows = ML_AZ * pieces
+    stride_rows = ML_AZ * own_blocks
+
+    def strip_of(ref, strip):
+        lo, hi = cuts[strip], cuts[strip + 1]
+        return ref.at[pl.ds(lo, hi - lo)]
+
+    def source(target, strip):
+        lo, hi = cuts[strip], cuts[strip + 1]
+        begin = pl.multiple_of(lax.rem(target, n_rg) * stride_rows + lo, 16)
+        return data.at[target // n_rg, pl.ds(begin, hi - lo)]
+
+    def data_copy(target, strip):
         return pltpu.make_async_remote_copy(
-            src_ref=data_ref.at[target], dst_ref=recv.at[me],
-            send_sem=send_sem.at[target], recv_sem=recv_sem.at[me],
+            src_ref=source(target, strip), dst_ref=strip_of(recv.at[me], strip),
+            send_sem=send_sem.at[strip, target], recv_sem=recv_sem.at[strip, me],
             device_id={"date": target}, device_id_type=pl.DeviceIdType.MESH,
         )
 
     def flag_copy(target):
         return pltpu.make_async_remote_copy(
-            src_ref=flags_ref, dst_ref=flags.at[me + SPAN],
+            src_ref=own_flags, dst_ref=flags.at[me + SPAN],
             send_sem=fsend_sem.at[target], recv_sem=frecv_sem.at[me],
             device_id={"date": target}, device_id_type=pl.DeviceIdType.MESH,
         )
 
-    def send(i, carry):
+    for strip in range(2):
+        pltpu.make_async_copy(
+            source(me, strip), strip_of(recv.at[me], strip), recv_sem.at[strip, me]
+        ).start()
+    pltpu.make_async_copy(own_flags, flags.at[me + SPAN], frecv_sem.at[me]).start()
+
+    pl.semaphore_wait(barrier, n - 1)
+
+    def send_first(i, carry):
         target = lax.rem(me + i, n)
+        data_copy(target, 0).start()
         flag_copy(target).start()
-        data_copy(target, 0).start()
-        return carry
-
-    lax.fori_loop(1, n, send, 0)
+        return carry
+
+    lax.fori_loop(1, n, send_first, 0)
+
+    def send_second(i, carry):
+        data_copy(lax.rem(me + i, n), 1).start()
+        return carry
+
+    lax.fori_loop(1, n, send_second, 0)
 
     k_id = lax.broadcasted_iota(jnp.int32, (LANES, LANES), 0)
     j_id = lax.broadcasted_iota(jnp.int32, (LANES, LANES), 1)
     circ = []
     for m in range(4):
         base = jnp.broadcast_to(taps_ref[m:m + 1, :], (LANES, LANES))
-        circ.append(pltpu.roll(base, 0, 1, stride=1, stride_axis=0))
+        circ.append(pltpu.roll(base, 0, 1, stride=1, stride_axis=0).T)
     for half in range(2):
         keep = (j_id <= k_id) if half == 0 else (j_id > k_id)
         for band in range(2):
@@ -98,7 +159,7 @@
             mat[128:256, col:col + 128] = im_minus
             mat[128:256, col + 128:col + 256] = re_part
 
-    for ref in (bands, power, raw_w, raw_n, wgt, phs, phi_a, phi_b):
+    for ref in (raw_w, raw_n, wgt, phs, phi_a, phi_b):
         ref[...] = jnp.zeros_like(ref)
     flags[0:SPAN] = jnp.zeros((SPAN,) + flags.shape[1:], F32)
 
@@ -117,25 +178,39 @@
 
     ring = bands.shape[0]
 
-    def one_date(d, carry):
-        pltpu.make_async_copy(recv.at[d], recv.at[d], recv_sem.at[d]).wait()
+    def one_date(strip, d):
+        r0, r1 = cuts[strip], cuts[strip + 1]
+        first = max(r0 - ML_AZ, 0)
+        b0 = first // ML_AZ
+        count = (r1 - first) // ML_AZ - 1
+        pad = -(-count // 8) * 8
         pltpu.make_async_copy(
-            flags.at[d + SPAN], flags.at[d + SPAN], frecv_sem.at[d]
+            strip_of(recv.at[d], strip), strip_of(recv.at[d], strip), recv_sem.at[strip, d]
         ).wait()
-        filt[...] = jnp.dot(recv[d], mat[...], preferred_element_type=F32)
+        if strip == 0:
+            pltpu.make_async_copy(
+                flags.at[d + SPAN], flags.at[d + SPAN], frecv_sem.at[d]
+            ).wait()
+        base = first // 16 * 16
+        off = first - base
+        made = jnp.dot(recv[d, base:r1], mat[...], preferred_element_type=F32)
+        for g in range(8):
+            filt[g, 0:r1 - base, :] = made[:, g * LANES:g * LANES + LANES]
         slot = lax.rem(d, ring)
         for r in range(ML_AZ):
-            first = r * pieces
-            value = filt[first:first + blocks, 0:512] + filt[first + 1:first + 1 + blocks, 512:1024]
-            bands[slot, r, 0:blocks, :] = value.astype(BF16).astype(F32)
+            for g in range(4):
+                low = filt[g, pl.ds(off + r, count, stride=ML_AZ), :]
+                high = filt[g + 4, pl.ds(off + r + ML_AZ, count, stride=ML_AZ), :]
+                value = (low + high).astype(BF16).astype(F32)
+                bands[slot, r, 0:count, g * LANES:g * LANES + LANES] = value
         new_power = []
         for band in range(2):
             total = None
             for r in range(ML_AZ):
-                value = bands[slot, r, :, band * 256:band * 256 + 256]
+                value = bands[slot, r, 0:pad, band * 256:band * 256 + 256]
                 total = value * value if total is None else total + value * value
             new_power.append(looks(total, sum_re))
-            power[slot, band, :, 0:rows_pad] = new_power[band]
+            power[slot, band, :, 0:pad] = new_power[band]
         for k in range(1, SPAN + 1):
             early = lax.rem(d + ring - k, ring)
             cross = []
@@ -143,23 +218,30 @@
                 total_re = None
                 total_im = None
                 for r in range(ML_AZ):
-                    a = bands[early, r, :, band * 256:band * 256 + 256]
-                    b = bands[slot, r, :, band * 256:band * 256 + 256]
+                    a = bands[early, r, 0:pad, band * 256:band * 256 + 256]
+                    b = bands[slot, r, 0:pad, band * 256:band * 256 + 256]
                     b_swap = jnp.concatenate([b[:, 128:], b[:, :128]], axis=1)
                     total_re = a * b if total_re is None else total_re + a * b
                     total_im = a * b_swap if total_im is None else total_im + a * b_swap
                 cross.append((looks(total_re, sum_re), looks(total_im, sum_im)))
             (cr0, ci0), (cr1, ci1) = cross
-            ab0 = power[early, 0, :, 0:rows_pad] * new_power[0] + eps_power
-            ab1 = power[early, 1, :, 0:rows_pad] * new_power[1] + eps_power
-            flag = flags[d - k + SPAN, k - 1:k, 0:rows_pad]
+            ab0 = power[early, 0, :, 0:pad] * new_power[0] + eps_power
+            ab1 = power[early, 1, :, 0:pad] * new_power[1] + eps_power
+            flag = flags[d - k + SPAN, k - 1:k, 0:pad]
             weight = flag * 0.5 * ((cr0 * cr0 + ci0 * ci0) / ab0 + (cr1 * cr1 + ci1 * ci1) / ab1)
             phase = split_coef * (ci0 * cr1 - cr0 * ci1) / jnp.sqrt(ab0 * ab1)
-            raw_w[k - 1, d - k + SPAN, :, 0:rows_pad] = weight
-            raw_n[k - 1, d - k + SPAN, :, 0:rows_pad] = weight * phase
-        return carry
-
-    lax.fori_loop(0, n, one_date, 0)
+            raw_w[k - 1, d - k + SPAN, :, b0:b0 + count] = weight[:, 0:count]
+            raw_n[k - 1, d - k + SPAN, :, b0:b0 + count] = (weight * phase)[:, 0:count]
+
+    for strip in range(2):
+        bands[...] = jnp.zeros_like(bands)
+        power[...] = jnp.zeros_like(power)
+
+        def step_date(d, carry):
+            one_date(strip, d)
+            return carry
+
+        lax.fori_loop(0, n, step_date, 0)
 
     step = min(8, n)
     shape = (step, CELLS, LANES)
@@ -256,6 +338,7 @@
     def drain(i, carry):
         target = lax.rem(me + i, n)
         data_copy(target, 0).wait_send()
+        data_copy(target, 1).wait_send()
         flag_copy(target).wait_send()
         out_copy(target).wait_send()
         return carry
@@ -280,34 +363,29 @@
     rows_pad = -(-(pieces - 1) // 8) * 8
     chunk_rows = ML_AZ * pieces
 
-    x = slc_stack[0].reshape(2, n_az, ML_AZ, span // LANES, LANES).transpose(1, 2, 3, 0, 4)
-    x = jnp.pad(x, ((0, 0), (0, 0), (2, 2), (0, 0), (0, 0)))
-    chunks = [x[:, :, q * own_blocks:q * own_blocks + pieces] for q in range(n_rg)]
-    data = jnp.stack(chunks, axis=1).reshape(n, chunk_rows, 2 * LANES)
-
-    flags = jnp.broadcast_to(
-        jnp.pad(pair_flags[0].astype(F32), (0, 8 - SPAN))[:, None], (8, LANES)
-    )
-    h = band_taps.astype(F32).reshape(4, TAPS)
-    taps = jnp.concatenate(
-        [h[:, :1], jnp.zeros((4, LANES - TAPS), F32), jnp.flip(h[:, 1:], axis=1)], axis=1
-    )
-    taps = jnp.pad(taps, ((0, 4), (0, 0)))
+    half = -(-chunk_rows // 32) * 16
+    cuts = (0, half, chunk_rows)
+    taps = jnp.pad(band_taps.astype(F32).reshape(4, TAPS), ((0, 4), (0, LANES - TAPS)))
+    padded_rows = ML_AZ * (span // LANES + 4)
 
     vmem = pl.BlockSpec(memory_space=pltpu.VMEM)
     small = lambda *lead: pltpu.VMEM((*lead, CELLS, LANES), F32)
     ring = SPAN + 1
     sem = pltpu.SemaphoreType.DMA((n,))
+    two_sem = pltpu.SemaphoreType.DMA((2, n))
     back = pl.pallas_call(
-        functools.partial(kernel, n, n_rg, pieces),
+        functools.partial(kernel, n, n_rg, pieces, cuts),
         out_shape=jax.ShapeDtypeStruct((n, CELLS, LANES), F32),
-        in_specs=[vmem] * 3,
+        in_specs=[pl.BlockSpec(memory_space=pl.ANY), vmem, vmem],
         out_specs=vmem,
         scratch_shapes=[
+            pltpu.VMEM((2, rows, span), BF16),
+            pltpu.VMEM((n_az, padded_rows, 2 * LANES), BF16),
+            pltpu.VMEM((8, LANES), F32),
             pltpu.VMEM((n, chunk_rows, 2 * LANES), BF16),
             small(n + SPAN),
             pltpu.VMEM((256, 1024), BF16),
-            pltpu.VMEM((chunk_rows, 1024), F32),
+            pltpu.VMEM((8, chunk_rows, LANES), F32),
             pltpu.VMEM((ring, ML_AZ, rows_pad, 512), F32),
             small(ring, 2),
             small(SPAN, n + 2 * SPAN),
@@ -321,12 +399,12 @@
             small(n),
             small(n),
             small(n),
-            sem, sem, sem, sem, sem, sem,
+            pltpu.SemaphoreType.DMA, two_sem, two_sem, sem, sem, sem, sem,
         ],
         compiler_params=pltpu.CompilerParams(
             collective_id=0, has_side_effects=True, vmem_limit_bytes=48 * 1024 * 1024
         ),
-    )(data, flags, taps)
+    )(slc_stack, pair_flags, taps)
     outs = back.reshape(n_az, n_rg, CELLS, 2, LANES // 2)[..., :own_blocks]
     outs = outs.transpose(3, 0, 1, 4, 2).reshape(2, 1, n_az, span // ML_RG)
     return outs[0], outs[1]

time: 59 us -> 56.2 us (0.953)
  other arithmetic: 2.24 us -> 0.01 us
  local copies, waits for them, and re-layouts: 6.67 us -> 4.47 us
  Pallas kernels: 49.2 us -> 50.9 us
    another operation x1 -> x0, other arithmetic: 2.16 us -> none  [local(): data = jnp.stack(chunks, axis=1).reshape(n, chunk_rows, 2 * LANES)]
    another operation x2 -> x0, local copies, waits for them, and re-layouts: 2.14 us -> none  [the longest x1 1.08 us: local(): slc_stack[0].reshape(2, n_az, ML_AZ, span // LANES, LANES)]
    pallas_call x1, Pallas kernels: 49.2 us -> 50.9 us  [local(): pl.pallas_call(functools.partial(kernel, n, n_rg, pieces, cuts), out_shap...]
    unnamed x6 -> x7, local copies, waits for them, and re-layouts: 1.7 us -> 2.77 us
    reshape x1 -> x0, local copies, waits for them, and re-layouts: 0.79 us -> none  [local(): data = jnp.stack(chunks, axis=1).reshape(n, chunk_rows, 2 * LANES)]
where the time goes in v2:
time: 56.2 us; the launch traced here: 56 us
  Pallas kernels  50.9 us (91%)
  local copies, waits for them, and re-layouts  4.47 us (8%)
  between operations  0.67 us (1%)
    pallas_call x1, Pallas kernels, local(): pl.pallas_call(functools.partial(kernel, n, n_rg, pieces, cuts), out_shap...  50.9 us
    unnamed x7, local copies, waits for them, and re-layouts  2.77 us
    squeeze x2, local copies, waits for them, and re-layouts, local(): return (outs[0], outs[1])  1.53 us

profile of v2, /device:TPU:0, one launch (start us, length us, event | category | flops | bytes accessed | tf_op | source)
XLA Modules:
  0.0 56.0 jit_solution(4372340530509346816)
XLA Ops:
  0.6 0.0 copy-start.2
  0.6 0.7 %copy-done.2 = bf16[2,2,32]{2,1,0:T(2,128)(2,1)S(1)} copy-done((bf16[2,2,32]{2,1,0:T(2,128)(2,1)S(1)}, bf16[2,2,32]{2,1,0:T(2,128)(2,1)}, u32[]{:S(2)}) %copy-start.2) | copy-done | bytes 280
  1.3 0.0 copy-start.1
  1.3 0.6 %copy-done.1 = s32[1,4]{1,0:T(1,128)S(1)} copy-done((s32[1,4]{1,0:T(1,128)S(1)}, s32[1,4]{1,0:T(1,128)}, u32[]{:S(2)}) %copy-start.1) | copy-done | bytes 40
  2.0 0.0 copy-start
  2.0 1.2 %copy-done = bf16[1,2,16,16384]{3,2,1,0:T(8,128)(2,1)S(1)} copy-done((bf16[1,2,16,16384]{3,2,1,0:T(8,128)(2,1)S(1)}, bf16[1,2,16,16384]{3,2,1,0:T(8,128)(2,1)}, u32[]{:S(2)}) %copy-start) | copy-done | bytes 1048600
  3.2 50.9 %shard_map.50 = f32[16,8,128]{2,1,0:T(8,128)S(1)} custom-call(bf16[1,2,16,16384]{3,2,1,0:T(8,128)(2,1)S(1)} %copy-done, s32[1,4]{1,0:T(1,128)S(1)} %copy-done.1, f32[8,128]{1,0:T(8,128)S(1)} %pad_convert_fusion.taps_ref), custom_call_target="tpu_custom_call" | custom-call | tf_op jit(solution)/shard_map/pallas_call | solution.py:376
  54.1 0.1 reshape.17
  54.2 0.2 copy.8
  54.5 0.8 %squeeze.7 = f32[1,4,1024]{2,1,0:T(4,128)} reshape(f32[1,4,4,32,8]{4,3,2,1,0:T(8,128)S(1)} %get-tuple-element.2) | data formatting | bytes 32768 | tf_op jit(solution)/shard_map/squeeze | solution.py:410
  55.3 0.8 %squeeze.6 = f32[1,4,1024]{2,1,0:T(4,128)} reshape(f32[1,4,4,32,8]{4,3,2,1,0:T(8,128)S(1)} %get-tuple-element.3) | data formatting | bytes 32768 | tf_op jit(solution)/shard_map/squeeze | solution.py:410
  (2 shorter events, 0.0 us)
Async XLA Ops:
  0.6 0.7 %copy-start.2 = (bf16[2,2,32]{2,1,0:T(2,128)(2,1)S(1)}, bf16[2,2,32]{2,1,0:T(2,128)(2,1)}, u32[]{:S(2)}) copy-start(bf16[2,2,32]{2,1,0:T(2,128)(2,1)} %param.4) | copy-start | bytes 772
  1.3 0.7 %copy-start.1 = (s32[1,4]{1,0:T(1,128)S(1)}, s32[1,4]{1,0:T(1,128)}, u32[]{:S(2)}) copy-start(s32[1,4]{1,0:T(1,128)} %flags_in.1) | copy-start | bytes 52
  2.0 1.2 %copy-start = (bf16[1,2,16,16384]{3,2,1,0:T(8,128)(2,1)S(1)}, bf16[1,2,16,16384]{3,2,1,0:T(8,128)(2,1)}, u32[]{:S(2)}) copy-start(bf16[1,2,16,16384]{3,2,1,0:T(8,128)(2,1)} %slc_ref.1) | copy-start | bytes 3145732

commit v3 on v2

--- a/solution.py
+++ b/solution.py
@@ -28,8 +28,8 @@
 
 def kernel(
     n, n_rg, pieces, cuts,
-    slc_ref, flags_in, taps_ref, out_ref,
-    slc, data, own_flags, recv, flags, mat, filt, bands, power, raw_w, raw_n, wgt, phs, phi_a, phi_b,
+    slc_hbm, flags_hbm, taps_hbm, phase_out, total_out,
+    slc, flags_in, taps_in, taps_ref, data, own_flags, recv, flags, mat, filt, bands, power, cross, wgt, phs, phi_a, phi_b,
     rhs, inv, wsum, pack, back,
     in_sem, send_sem, recv_sem, fsend_sem, frecv_sem, osend_sem, orecv_sem,
 ):
@@ -39,6 +39,12 @@
     rows_pad = bands.shape[2]
     my_q = lax.rem(me, n_rg)
 
+    slc_load = pltpu.make_async_copy(slc_hbm.at[0], slc, in_sem.at[0])
+    slc_load.start()
+    flags_load = pltpu.make_async_copy(flags_hbm, flags_in, in_sem.at[1])
+    flags_load.start()
+    taps_load = pltpu.make_async_copy(taps_hbm, taps_in, in_sem.at[2])
+    taps_load.start()
     barrier = pltpu.get_barrier_semaphore()
 
     def greet(i, carry):
@@ -50,14 +56,14 @@
 
     lax.fori_loop(1, n, greet, 0)
 
-    load = pltpu.make_async_copy(slc_ref.at[0], slc, in_sem)
-    load.start()
-
-    row_8 = lax.broadcasted_iota(jnp.int32, (8, 4), 0)
-    col_8 = lax.broadcasted_iota(jnp.int32, (8, 4), 1)
-    picked = jnp.where(row_8 == col_8, flags_in[...].astype(F32), 0.0)
-    own_flags[...] = jnp.broadcast_to(jnp.sum(picked, axis=1, keepdims=True), (8, LANES))
-    load.wait()
+    flags_load.wait()
+    own_flags[...] = jnp.zeros_like(own_flags)
+    own_flags[0:1, 0:SPAN] = flags_in[...].astype(F32)
+    taps_load.wait()
+    taps_ref[...] = jnp.zeros_like(taps_ref)
+    for band in range(2):
+        taps_ref[2 * band:2 * band + 2, 0:TAPS] = taps_in[band].astype(F32)
+    slc_load.wait()
 
     n_az = n // n_rg
     n_tiles = data.shape[1] // 16
@@ -126,19 +132,20 @@
 
     pl.semaphore_wait(barrier, n - 1)
 
-    def send_first(i, carry):
-        target = lax.rem(me + i, n)
-        data_copy(target, 0).start()
-        flag_copy(target).start()
-        return carry
-
-    lax.fori_loop(1, n, send_first, 0)
-
-    def send_second(i, carry):
-        data_copy(lax.rem(me + i, n), 1).start()
-        return carry
-
-    lax.fori_loop(1, n, send_second, 0)
+    def send_strip(strip):
+        def send_pair(i, carry):
+            for target, go in ((n - 1 - i, n - 1 - i > me), (i, i < me)):
+                @pl.when(go)
+                def _():
+                    data_copy(target, strip).start()
+                    if strip == 0:
+                        flag_copy(target).start()
+            return carry
+
+        lax.fori_loop(0, n, send_pair, 0)
+
+    send_strip(0)
+    send_strip(1)
 
     k_id = lax.broadcasted_iota(jnp.int32, (LANES, LANES), 0)
     j_id = lax.broadcasted_iota(jnp.int32, (LANES, LANES), 1)
@@ -159,7 +166,7 @@
             mat[128:256, col:col + 128] = im_minus
             mat[128:256, col + 128:col + 256] = re_part
 
-    for ref in (raw_w, raw_n, wgt, phs, phi_a, phi_b):
+    for ref in (bands, power, cross, wgt, phs, phi_a, phi_b):
         ref[...] = jnp.zeros_like(ref)
     flags[0:SPAN] = jnp.zeros((SPAN,) + flags.shape[1:], F32)
 
@@ -178,70 +185,80 @@
 
     ring = bands.shape[0]
 
-    def one_date(strip, d):
+    group = 4 if n % 4 == 0 else 1
+
+    def some_dates(strip, i):
         r0, r1 = cuts[strip], cuts[strip + 1]
         first = max(r0 - ML_AZ, 0)
         b0 = first // ML_AZ
         count = (r1 - first) // ML_AZ - 1
         pad = -(-count // 8) * 8
-        pltpu.make_async_copy(
-            strip_of(recv.at[d], strip), strip_of(recv.at[d], strip), recv_sem.at[strip, d]
-        ).wait()
-        if strip == 0:
-            pltpu.make_async_copy(
-                flags.at[d + SPAN], flags.at[d + SPAN], frecv_sem.at[d]
-            ).wait()
         base = first // 16 * 16
         off = first - base
-        made = jnp.dot(recv[d, base:r1], mat[...], preferred_element_type=F32)
+        high_rows = r1 - base
+        for u in range(group):
+            d = i * group + u
+            pltpu.make_async_copy(
+                strip_of(recv.at[d], strip), strip_of(recv.at[d], strip), recv_sem.at[strip, d]
+            ).wait()
+            if strip == 0:
+                pltpu.make_async_copy(
+                    flags.at[d + SPAN], flags.at[d + SPAN], frecv_sem.at[d]
+                ).wait()
+        pieces_in = [recv[i * group + u, base:r1] for u in range(group)]
+        made = jnp.dot(
+            jnp.concatenate(pieces_in, axis=0), mat[...], preferred_element_type=F32
+        )
         for g in range(8):
-            filt[g, 0:r1 - base, :] = made[:, g * LANES:g * LANES + LANES]
-        slot = lax.rem(d, ring)
-        for r in range(ML_AZ):
-            for g in range(4):
-                low = filt[g, pl.ds(off + r, count, stride=ML_AZ), :]
-                high = filt[g + 4, pl.ds(off + r + ML_AZ, count, stride=ML_AZ), :]
-                value = (low + high).astype(BF16).astype(F32)
-                bands[slot, r, 0:count, g * LANES:g * LANES + LANES] = value
-        new_power = []
-        for band in range(2):
-            total = None
+            filt[g, 0:group * high_rows, :] = made[:, g * LANES:g * LANES + LANES]
+        for u in range(group):
+            slot = lax.rem(i * group + u, ring)
             for r in range(ML_AZ):
-                value = bands[slot, r, 0:pad, band * 256:band * 256 + 256]
-                total = value * value if total is None else total + value * value
-            new_power.append(looks(total, sum_re))
-            power[slot, band, :, 0:pad] = new_power[band]
-        for k in range(1, SPAN + 1):
-            early = lax.rem(d + ring - k, ring)
-            cross = []
+                for g in range(4):
+                    start = u * high_rows + off + r
+                    low = filt[g, pl.ds(start, count, stride=ML_AZ), :]
+                    high = filt[g + 4, pl.ds(start + ML_AZ, count, stride=ML_AZ), :]
+                    value = (low + high).astype(BF16).astype(F32)
+                    bands[slot, r, 0:count, g * LANES:g * LANES + LANES] = value
+        for u in range(group):
+            d = i * group + u
+            slot = lax.rem(d, ring)
+            re_list = []
+            im_list = []
             for band in range(2):
-                total_re = None
-                total_im = None
-                for r in range(ML_AZ):
-                    a = bands[early, r, 0:pad, band * 256:band * 256 + 256]
-                    b = bands[slot, r, 0:pad, band * 256:band * 256 + 256]
-                    b_swap = jnp.concatenate([b[:, 128:], b[:, :128]], axis=1)
-                    total_re = a * b if total_re is None else total_re + a * b
-                    total_im = a * b_swap if total_im is None else total_im + a * b_swap
-                cross.append((looks(total_re, sum_re), looks(total_im, sum_im)))
-            (cr0, ci0), (cr1, ci1) = cross
-            ab0 = power[early, 0, :, 0:pad] * new_power[0] + eps_power
-            ab1 = power[early, 1, :, 0:pad] * new_power[1] + eps_power
-            flag = flags[d - k + SPAN, k - 1:k, 0:pad]
-            weight = flag * 0.5 * ((cr0 * cr0 + ci0 * ci0) / ab0 + (cr1 * cr1 + ci1 * ci1) / ab1)
-            phase = split_coef * (ci0 * cr1 - cr0 * ci1) / jnp.sqrt(ab0 * ab1)
-            raw_w[k - 1, d - k + SPAN, :, b0:b0 + count] = weight[:, 0:count]
-            raw_n[k - 1, d - k + SPAN, :, b0:b0 + count] = (weight * phase)[:, 0:count]
+                cols = slice(band * 256, band * 256 + 256)
+                for k in range(SPAN + 1):
+                    early = lax.rem(d + ring - k, ring)
+                    total_re = None
+                    total_im = None
+                    for r in range(ML_AZ):
+                        a = bands[early, r, 0:pad, cols]
+                        b = bands[slot, r, 0:pad, cols]
+                        total_re = a * b if r == 0 else total_re + a * b
+                        if k > 0:
+                            b_swap = jnp.concatenate([b[:, 128:], b[:, :128]], axis=1)
+                            total_im = a * b_swap if r == 0 else total_im + a * b_swap
+                    re_list.append(total_re)
+                    if k > 0:
+                        im_list.append(total_im)
+            re_looks = looks(jnp.concatenate(re_list, axis=0), sum_re)
+            im_looks = looks(jnp.concatenate(im_list, axis=0), sum_im)
+            for band in range(2):
+                at = band * (SPAN + 1) * pad
+                power[band, d + SPAN, :, b0:b0 + count] = re_looks[:, at:at + count]
+                for k in range(1, SPAN + 1):
+                    at = (band * (SPAN + 1) + k) * pad
+                    cross[k - 1, 2 * band, d - k + SPAN, :, b0:b0 + count] = re_looks[:, at:at + count]
+                    at = (band * SPAN + k - 1) * pad
+                    cross[k - 1, 2 * band + 1, d - k + SPAN, :, b0:b0 + count] = im_looks[:, at:at + count]
 
     for strip in range(2):
-        bands[...] = jnp.zeros_like(bands)
-        power[...] = jnp.zeros_like(power)
-
-        def step_date(d, carry):
-            one_date(strip, d)
+
+        def step_dates(i, carry):
+            some_dates(strip, i)
             return carry
 
-        lax.fori_loop(0, n, step_date, 0)
+        lax.fori_loop(0, n // group, step_dates, 0)
 
     step = min(8, n)
     shape = (step, CELLS, LANES)
@@ -259,11 +276,19 @@
         suffix = whole - prefix + value
         return pltpu.roll(suffix, 1, 2) + whole + pltpu.roll(prefix, LANES - 1, 2)
 
+    f_lane = lax.broadcasted_iota(jnp.int32, (step, 1, LANES), 2)
+
     def smooth(i, carry):
         at = i * step + SPAN
         for k in range(SPAN):
-            den = box(raw_w[k, pl.ds(at, step)])
-            num = box(raw_n[k, pl.ds(at, step)])
+            cr0, ci0, cr1, ci1 = (cross[k, m, pl.ds(at, step)] for m in range(4))
+            ab0 = power[0, pl.ds(at, step)] * power[0, pl.ds(at + k + 1, step)] + eps_power
+            ab1 = power[1, pl.ds(at, step)] * power[1, pl.ds(at + k + 1, step)] + eps_power
+            flag = jnp.sum(jnp.where(f_lane == k, flags[pl.ds(at, step)], 0.0), axis=2, keepdims=True)
+            weight = flag * 0.5 * ((cr0 * cr0 + ci0 * ci0) / ab0 + (cr1 * cr1 + ci1 * ci1) / ab1)
+            phase = split_coef * (ci0 * cr1 - cr0 * ci1) / jnp.sqrt(ab0 * ab1)
+            den = box(weight)
+            num = box(weight * phase)
             phs[k, pl.ds(at, step)] = num / (den + floor_weight)
             wgt[k, pl.ds(at, step)] = den / (2 * RADIUS + 1)
         return carry
@@ -347,10 +372,33 @@
 
     def arrive(s, carry):
         pltpu.make_async_copy(back.at[s], back.at[s], orecv_sem.at[s]).wait()
-        out_ref[s] = back[s]
         return carry
 
     lax.fori_loop(0, n, arrive, 0)
+
+    wide = own_blocks * CELLS
+    value = back[...].reshape(n * CELLS, LANES)
+    high = value.astype(BF16)
+    rest = value - high.astype(F32)
+    middle = rest.astype(BF16)
+    low = (rest - middle.astype(F32)).astype(BF16)
+    place_row = lax.broadcasted_iota(jnp.int32, (LANES, 2 * wide), 0)
+    place_col = lax.broadcasted_iota(jnp.int32, (LANES, 2 * wide), 1)
+    place_row_of = (place_col // wide) * 64 + lax.rem(place_col, wide) // CELLS
+    place = jnp.where(place_row == place_row_of, 1.0, 0.0).astype(BF16)
+    spread = jnp.dot(
+        jnp.concatenate([high, middle, low], axis=0), place, preferred_element_type=F32
+    )
+    count = n * CELLS
+    spread = spread[0:count] + spread[count:2 * count] + spread[2 * count:3 * count]
+    spread = spread.reshape(n, CELLS, 2 * wide)
+    s_row = lax.broadcasted_iota(jnp.int32, spread.shape, 1)
+    s_col = lax.broadcasted_iota(jnp.int32, spread.shape, 2)
+    rows = jnp.sum(jnp.where(lax.rem(s_col, CELLS) == s_row, spread, 0.0), axis=1)
+    for s in range(n):
+        az, q = s // n_rg, s % n_rg
+        phase_out[az:az + 1, q * wide:q * wide + wide] = rows[s:s + 1, 0:wide]
+        total_out[az:az + 1, q * wide:q * wide + wide] = rows[s:s + 1, wide:2 * wide]
 
 
 def local(slc_stack, band_taps, pair_flags):
@@ -365,31 +413,32 @@
 
     half = -(-chunk_rows // 32) * 16
     cuts = (0, half, chunk_rows)
-    taps = jnp.pad(band_taps.astype(F32).reshape(4, TAPS), ((0, 4), (0, LANES - TAPS)))
     padded_rows = ML_AZ * (span // LANES + 4)
 
     vmem = pl.BlockSpec(memory_space=pltpu.VMEM)
     small = lambda *lead: pltpu.VMEM((*lead, CELLS, LANES), F32)
-    ring = SPAN + 1
+    ring = 2 * SPAN
     sem = pltpu.SemaphoreType.DMA((n,))
     two_sem = pltpu.SemaphoreType.DMA((2, n))
-    back = pl.pallas_call(
+    phase, total = pl.pallas_call(
         functools.partial(kernel, n, n_rg, pieces, cuts),
-        out_shape=jax.ShapeDtypeStruct((n, CELLS, LANES), F32),
-        in_specs=[pl.BlockSpec(memory_space=pl.ANY), vmem, vmem],
-        out_specs=vmem,
+        out_shape=[jax.ShapeDtypeStruct((n_az, span // ML_RG), F32)] * 2,
+        in_specs=[pl.BlockSpec(memory_space=pl.ANY)] * 3,
+        out_specs=[vmem] * 2,
         scratch_shapes=[
             pltpu.VMEM((2, rows, span), BF16),
+            pltpu.VMEM((1, SPAN), jnp.int32),
+            pltpu.VMEM((2, 2, TAPS), BF16),
+            pltpu.VMEM((8, LANES), F32),
             pltpu.VMEM((n_az, padded_rows, 2 * LANES), BF16),
-            pltpu.VMEM((8, LANES), F32),
+            pltpu.VMEM((1, LANES), F32),
             pltpu.VMEM((n, chunk_rows, 2 * LANES), BF16),
-            small(n + SPAN),
+            pltpu.VMEM((n + SPAN, 1, LANES), F32),
             pltpu.VMEM((256, 1024), BF16),
-            pltpu.VMEM((8, chunk_rows, LANES), F32),
+            pltpu.VMEM((8, 4 * chunk_rows, LANES), F32),
             pltpu.VMEM((ring, ML_AZ, rows_pad, 512), F32),
-            small(ring, 2),
-            small(SPAN, n + 2 * SPAN),
-            small(SPAN, n + 2 * SPAN),
+            small(2, n + 2 * SPAN),
+            small(SPAN, 4, n + 2 * SPAN),
             small(SPAN, n + 2 * SPAN),
             small(SPAN, n + 2 * SPAN),
             small(n + 2 * SPAN),
@@ -399,15 +448,13 @@
             small(n),
             small(n),
             small(n),
-            pltpu.SemaphoreType.DMA, two_sem, two_sem, sem, sem, sem, sem,
+            pltpu.SemaphoreType.DMA((3,)), two_sem, two_sem, sem, sem, sem, sem,
         ],
         compiler_params=pltpu.CompilerParams(
-            collective_id=0, has_side_effects=True, vmem_limit_bytes=48 * 1024 * 1024
+            collective_id=0, has_side_effects=True, vmem_limit_bytes=60 * 1024 * 1024
         ),
-    )(slc_stack, pair_flags, taps)
-    outs = back.reshape(n_az, n_rg, CELLS, 2, LANES // 2)[..., :own_blocks]
-    outs = outs.transpose(3, 0, 1, 4, 2).reshape(2, 1, n_az, span // ML_RG)
-    return outs[0], outs[1]
+    )(slc_stack, pair_flags, band_taps)
+    return phase[None], total[None]
 
 
 def solution(mesh):

time: 56.2 us -> 46.3 us (0.82)
  Pallas kernels: 50.9 us -> 43.6 us
  local copies, waits for them, and re-layouts: 4.47 us -> 1.94 us
    pallas_call x1, Pallas kernels: 50.9 us -> 43.6 us  [local(): pl.pallas_call(functools.partial(kernel, n, n_rg, pieces, cuts), out_shap...]
    squeeze x2 -> x0, local copies, waits for them, and re-layouts: 1.53 us -> none  [local(): return (outs[0], outs[1])]
    unnamed x7 -> x4, local copies, waits for them, and re-layouts: 2.77 us -> 1.94 us
where the time goes in v3:
time: 46.3 us; the launch traced here: 46.1 us
  Pallas kernels  43.6 us (94%)
  local copies, waits for them, and re-layouts  1.94 us (4%)
  between operations  0.65 us (1%)
    pallas_call x1, Pallas kernels, local(): pl.pallas_call(functools.partial(kernel, n, n_rg, pieces, cuts), out_shap...  43.6 us
    unnamed x4, local copies, waits for them, and re-layouts  1.94 us

profile of v3, /device:TPU:0, one launch (start us, length us, event | category | flops | bytes accessed | tf_op | source)
XLA Modules:
  0.0 46.1 jit_solution(2345116883867591000)
XLA Ops:
  0.6 43.6 %shard_map.50 = (f32[4,1024]{1,0:T(4,128)}, f32[4,1024]{1,0:T(4,128)}) custom-call(bf16[1,2,16,16384]{3,2,1,0:T(8,128)(2,1)} %slc_hbm.1, s32[1,4]{1,0:T(1,128)} %flags_hbm.1, bf16[2,2,32]{2,1,0:T(2,128)(2,1)} %taps_hbm.1), custom_call_target="tpu_custom_call" | custom-call | tf_op jit(solution)/shard_map/pallas_call | solution.py:423
  44.2 0.0 copy-start
  44.2 1.3 %copy.7 = f32[1,4,1024]{2,1,0:T(4,128)} copy(f32[1,4,1024]{2,1,0:T(4,128)} %bitcast.3) | data formatting | bytes 32768
  45.5 0.0 copy-done
  45.5 0.6 %copy.8 = f32[1,4,1024]{2,1,0:T(4,128)} copy(f32[1,4,1024]{2,1,0:T(4,128)S(1)} %bitcast.2) | data formatting | bytes 32768
Async XLA Ops:
  44.2 1.3 %copy-start = (f32[4,1024]{1,0:T(4,128)S(1)}, f32[4,1024]{1,0:T(4,128)}, u32[]{:S(2)}) copy-start(f32[4,1024]{1,0:T(4,128)} %get-tuple-element.5) | copy-start | bytes 49156

commit v4 on v3

--- a/solution.py
+++ b/solution.py
@@ -28,7 +28,7 @@
 
 def kernel(
     n, n_rg, pieces, cuts,
-    slc_hbm, flags_hbm, taps_hbm, phase_out, total_out,
+    slc_hbm, flags_hbm, taps_hbm, out_ref,
     slc, flags_in, taps_in, taps_ref, data, own_flags, recv, flags, mat, filt, bands, power, cross, wgt, phs, phi_a, phi_b,
     rhs, inv, wsum, pack, back,
     in_sem, send_sem, recv_sem, fsend_sem, frecv_sem, osend_sem, orecv_sem,
@@ -397,8 +397,8 @@
     rows = jnp.sum(jnp.where(lax.rem(s_col, CELLS) == s_row, spread, 0.0), axis=1)
     for s in range(n):
         az, q = s // n_rg, s % n_rg
-        phase_out[az:az + 1, q * wide:q * wide + wide] = rows[s:s + 1, 0:wide]
-        total_out[az:az + 1, q * wide:q * wide + wide] = rows[s:s + 1, wide:2 * wide]
+        out_ref[0, az:az + 1, q * wide:q * wide + wide] = rows[s:s + 1, 0:wide]
+        out_ref[1, az:az + 1, q * wide:q * wide + wide] = rows[s:s + 1, wide:2 * wide]
 
 
 def local(slc_stack, band_taps, pair_flags):
@@ -420,11 +420,11 @@
     ring = 2 * SPAN
     sem = pltpu.SemaphoreType.DMA((n,))
     two_sem = pltpu.SemaphoreType.DMA((2, n))
-    phase, total = pl.pallas_call(
+    both = pl.pallas_call(
         functools.partial(kernel, n, n_rg, pieces, cuts),
-        out_shape=[jax.ShapeDtypeStruct((n_az, span // ML_RG), F32)] * 2,
+        out_shape=jax.ShapeDtypeStruct((2, n_az, span // ML_RG), F32),
         in_specs=[pl.BlockSpec(memory_space=pl.ANY)] * 3,
-        out_specs=[vmem] * 2,
+        out_specs=vmem,
         scratch_shapes=[
             pltpu.VMEM((2, rows, span), BF16),
             pltpu.VMEM((1, SPAN), jnp.int32),
@@ -454,7 +454,7 @@
             collective_id=0, has_side_effects=True, vmem_limit_bytes=60 * 1024 * 1024
         ),
     )(slc_stack, pair_flags, band_taps)
-    return phase[None], total[None]
+    return both[0:1], both[1:2]
 
 
 def solution(mesh):

time: 46.3 us -> 45.8 us (0.989)
  local copies, waits for them, and re-layouts: 1.94 us -> 1.35 us
    unnamed x4 -> x0, local copies, waits for them, and re-layouts: 1.94 us -> none
    slice x0 -> x1, local copies, waits for them, and re-layouts: none -> 1.35 us  [local(): return (both[0:1], both[1:2])]
where the time goes in v4:
time: 45.8 us; the launch traced here: 45.6 us
  Pallas kernels  43.6 us (95%)
  local copies, waits for them, and re-layouts  1.35 us (3%)
  between operations  0.64 us (1%)
    pallas_call x1, Pallas kernels, local(): pl.pallas_call(functools.partial(kernel, n, n_rg, pieces, cuts), out_shap...  43.6 us
    slice x1, local copies, waits for them, and re-layouts, local(): return (both[0:1], both[1:2])  1.35 us

profile of v4, /device:TPU:0, one launch (start us, length us, event | category | flops | bytes accessed | tf_op | source)
XLA Modules:
  0.0 45.6 jit_solution(13474587668521934551)
XLA Ops:
  0.6 43.6 %shard_map.50 = f32[2,4,1024]{2,1,0:T(4,128)} custom-call(bf16[1,2,16,16384]{3,2,1,0:T(8,128)(2,1)} %slc_hbm.1, s32[1,4]{1,0:T(1,128)} %flags_hbm.1, bf16[2,2,32]{2,1,0:T(2,128)(2,1)} %taps_hbm.1), custom_call_target="tpu_custom_call" | custom-call | tf_op jit(solution)/shard_map/pallas_call | solution.py:423
  44.2 1.3 %fusion = (f32[1,4,1024]{2,1,0:T(4,128)}, f32[1,4,1024]{2,1,0:T(4,128)}) fusion(f32[2,4,1024]{2,1,0:T(4,128)} %shard_map.50), kind=kLoop, calls=%fused_computation | loop fusion | bytes 65536 | tf_op jit(solution)/shard_map/slice | solution.py:457
